TPU v7x, 32 devices: a whole 2x2x4 slice. The times are simulated.
32 devices in a mesh: rows: 8 (over y, x, core), heads: 4 (over z).
Axes of the slice: x: 2, y: 2, z: 4, core: 2. Of those that a mesh axis runs over, the one named last changes fastest.
Arguments:
- tokens: bfloat16 [32768, 768], P(('rows', 'heads')), may hold values from -6 to 6
- block_kind: int32 [64], P('rows'), may hold values from 0 to 2, as said below
- query_weight: bfloat16 [768, 768], P('rows', 'heads'), may hold values from -0.4375 to 0.4375
- key_weight: bfloat16 [768, 768], P('rows', 'heads'), may hold values from -0.21875 to 0.21875
- value_weight: bfloat16 [768, 768], P('rows', 'heads'), may hold values from -0.21875 to 0.21875
- query_bias: bfloat16 [768], replicated, may hold values from -4 to 4
- value_bias: bfloat16 [768], replicated, may hold values from -2 to 2
- output_weight: bfloat16 [768, 768], P(('rows', 'heads')), may hold values from -0.875 to 0.875
- output_bias: bfloat16 [768], replicated, may hold values from -2 to 2
- first_gain: bfloat16 [768], replicated, may hold values from 0.5 to 1.5
- first_shift: bfloat16 [768], replicated, may hold values from -2 to 2
- inner_weight: bfloat16 [768, 3072], P(('rows', 'heads')), may hold values from -0.21875 to 0.21875
- inner_bias: bfloat16 [3072], replicated, may hold values from -2 to 2
- outer_weight: bfloat16 [3072, 768], P(('rows', 'heads')), may hold values from -0.109375 to 0.109375
- outer_bias: bfloat16 [768], replicated, may hold values from -2 to 2
- second_gain: bfloat16 [768], replicated, may hold values from 0.5 to 1.5
- second_shift: bfloat16 [768], replicated, may hold values from -2 to 2
- cotangent: bfloat16 [32768, 768], P(('rows', 'heads')), may hold values from -6 to 6
Outputs:
- layer_out: bfloat16 [32768, 768], P(('rows', 'heads'))
- tokens_grad: float32 [32768, 768], P(('rows', 'heads'))
- query_weight_grad: float32 [768, 768], P('rows', 'heads')
- key_weight_grad: float32 [768, 768], P('rows', 'heads')
- value_weight_grad: float32 [768, 768], P('rows', 'heads')
- query_bias_grad: float32 [768], replicated
- value_bias_grad: float32 [768], replicated
- output_weight_grad: float32 [768, 768], P(('rows', 'heads'))
- output_bias_grad: float32 [768], replicated
- first_gain_grad: float32 [768], replicated
- first_shift_grad: float32 [768], replicated
- inner_weight_grad: float32 [768, 3072], P(('rows', 'heads'))
- inner_bias_grad: float32 [3072], replicated
- outer_weight_grad: float32 [3072, 768], P(('rows', 'heads'))
- outer_bias_grad: float32 [768], replicated
- second_gain_grad: float32 [768], replicated
- second_shift_grad: float32 [768], replicated
Inputs may be any that keep to these rules, and one draw needn't show every extreme that they name: `block_kind`: kind of each block of 512 tokens: 0 holds one sequence of 512 tokens, 1 holds four sequences of 128 tokens, 2 holds padding. Of the 8 blocks of one index of rows the padding ones come last, at most 4 of them.
All inputs are finite; a program needn't handle non-finite values.
Results may differ from a plain program's by a relative error of at most 0.015.
The roundings to bfloat16 on the way count: a program that leaves them out, or rounds other values in their place, can miss the bound.
Values may be sent and summed in bfloat16 or wider, within the bound.
No kernel may reach another device: no remote copies, remote signals or barrier semaphores. Data moves between devices by JAX's collectives and lax.ppermute only.
A program may use at most 192 MiB of HBM per device.

v0:
```python
import functools

import jax
import jax.numpy as jnp
from jax import lax
from jax.experimental import pallas as pl
from jax.experimental.pallas import tpu as pltpu
from jax.sharding import PartitionSpec as P

HEAD_DIM = 64
BLOCK = 512
PARTS = 4
EPSILON = 1e-06
SCALE = 0.125
F32 = jnp.float32
BF16 = jnp.bfloat16


def by_core(first, second):
    return jnp.where(lax.axis_index("rows") & 1 == 1, second, first)


SWAPS = {"core": (1, 1), "first": (2, 4), "second": (4, 2)}


def exchange(value, stage):
    bits = SWAPS[stage]
    return lax.ppermute(value, "rows", [(i, i ^ bits[i & 1]) for i in range(8)])


def shift_line(value, step):
    return lax.ppermute(value, "heads", [(i, (i + step) % 4) for i in range(4)])


def slot_orders():
    here = lax.axis_index("rows")
    first, second = by_core(2, 4), by_core(4, 2)
    keep = jnp.stack([here, here ^ first, here ^ second, here ^ 6])
    away = jnp.stack([here, here ^ second, here ^ first, here ^ 6]) ^ 1
    return keep.astype(jnp.int32), away.astype(jnp.int32)


def after(value, *others):
    return lax.optimization_barrier((value,) + others)[0]


def behind(value, gates):
    if not gates:
        return value
    values = value if isinstance(value, tuple) else (value,)
    values = lax.optimization_barrier(values + tuple(gates))[: len(values)]
    return values if isinstance(value, tuple) else values[0]


def line_gather(piece):
    return (piece,) + tuple(shift_line(piece, step) for step in (1, 2, 3))


def line_order(pieces):
    here = lax.axis_index("heads")
    turned = [pieces[-i % 4] for i in range(4)]
    for bit in (1, 2):
        turned = [
            jnp.where(here & bit == bit, turned[i - bit], turned[i]) for i in range(4)
        ]
    return jnp.stack(turned)


def plane_gather(piece):
    return exchange(piece, "first"), exchange(piece, "second")


def plane_rest(ones):
    return exchange(after(*ones), "second")


def core_gather(mine):
    return tuple(exchange(member, "core") for member in mine)


def scatter_steps(send, keep, stack):
    gates = yield send
    got = behind(exchange(send, "core"), gates)
    low = (keep[2:].astype(F32) + got[2:].astype(F32)).astype(BF16)
    gates = yield low
    got_two = behind(exchange(low, "second"), gates)
    one = (keep[1].astype(F32) + got[1].astype(F32) + got_two[1].astype(F32)).astype(BF16)
    gates = yield one
    got_one = behind(exchange(one, "first"), gates).astype(F32)
    zero = keep[0].astype(F32) + got[0].astype(F32) + got_two[0].astype(F32)
    stacked = stack((zero + got_one).astype(BF16))
    here = lax.axis_index("heads")
    sent = [
        lax.dynamic_index_in_dim(stacked, (here + step) % 4, keepdims=False)
        for step in range(4)
    ]
    gates = yield sent[3]
    parts = tuple(shift_line(sent[step], step) for step in (1, 2, 3))
    parts = behind(parts, gates)
    yield sent[0].astype(F32) + sum(part.astype(F32) for part in parts)


def stack_rows(part):
    return part.reshape(4, -1, part.shape[1])


def stack_columns(part):
    width = part.shape[1] // 12
    return part.reshape(-1, 3, 4, width).transpose(2, 0, 1, 3).reshape(4, -1, 3 * width)


def total_steps(value):
    value = value + exchange(value, "core")
    yield value
    value = value + exchange(value, "second")
    yield value
    value = value + exchange(value, "first")
    yield value
    yield value + sum(shift_line(value, step) for step in (1, 2, 3))


HBM = pl.BlockSpec(memory_space=pl.ANY)
WIDE = pltpu.CompilerParams(vmem_limit_bytes=50 << 20)


def copy_all(moves, semaphores):
    copies = [
        pltpu.make_async_copy(source, target, semaphores.at[i])
        for i, (source, target) in enumerate(moves)
    ]
    for copy in copies:
        copy.start()
    for copy in copies:
        copy.wait()


def project_kernel(order, tokens, bias, *refs):
    pieces, (packed, full, semaphores) = refs[:8], refs[8:]

    @pl.when(pl.program_id(0) == 0)
    def _():
        copy_all([(pieces[i], full.at[order[i]]) for i in range(8)], semaphores)

    weight = full[...].reshape(-1, full.shape[2])
    packed[...] = (dot_plain(tokens[...], weight) + bias[...]).astype(BF16)


def project(order, tokens, bias, pieces):
    count, width = tokens.shape
    depth, columns = pieces[0].shape
    tile = count // 4
    return pl.pallas_call(
        project_kernel,
        grid_spec=pltpu.PrefetchScalarGridSpec(
            num_scalar_prefetch=1,
            grid=(4,),
            in_specs=[
                pl.BlockSpec((tile, width), lambda i, *_: (i, 0)),
                pl.BlockSpec((1, columns), lambda i, *_: (0, 0)),
            ]
            + [HBM] * 8,
            out_specs=[
                pl.BlockSpec((tile, columns), lambda i, *_: (i, 0)),
                pl.BlockSpec((8, depth, columns), lambda i, *_: (0, 0, 0)),
            ],
            scratch_shapes=[pltpu.SemaphoreType.DMA((8,))],
        ),
        out_shape=(
            jax.ShapeDtypeStruct((count, columns), BF16),
            jax.ShapeDtypeStruct((8, depth, columns), BF16),
        ),
        compiler_params=WIDE,
        cost_estimate=pl.CostEstimate(
            flops=2 * count * width * columns,
            bytes_accessed=2 * (count * (width + columns) + 2 * width * columns),
            transcendentals=0,
        ),
        name="project",
    )(order, tokens, bias, *pieces)


def join_kernel(order, *refs):
    pieces, (output_full, inner_full, semaphores) = refs[:8], refs[8:]
    depth, width = output_full.shape[1:]
    moves = []
    for slot in range(8):
        moves.append((pieces[slot].at[pl.ds(0, depth)], output_full.at[order[slot]]))
        for column in range(inner_full.shape[2] // width):
            source = pieces[slot].at[pl.ds(depth * (1 + column), depth)]
            target = inner_full.at[order[slot], :, pl.ds(column * width, width)]
            moves.append((source, target))
    copy_all(moves, semaphores)


def join(order, pieces, depth, columns):
    width = pieces[0].shape[1]
    shapes = [(8, depth, width), (8, depth, columns * width)]
    size = pieces[0].size * 8
    return pl.pallas_call(
        join_kernel,
        in_specs=[pl.BlockSpec(memory_space=pltpu.SMEM)] + [HBM] * 8,
        out_specs=[pl.BlockSpec(memory_space=pltpu.VMEM)] * 2,
        out_shape=tuple(jax.ShapeDtypeStruct(shape, BF16) for shape in shapes),
        scratch_shapes=[pltpu.SemaphoreType.DMA((8 * (columns + 1),))],
        compiler_params=WIDE,
        cost_estimate=pl.CostEstimate(flops=0, bytes_accessed=4 * size, transcendentals=0),
        name="join",
    )(order, *pieces)


def rows_terms_kernel(parts, order, *refs):
    lefts, rights = refs[:parts], refs[parts : 2 * parts]
    send_ref, keep_ref, turned, product = refs[2 * parts :]
    step = pl.program_id(0)
    depth = send_ref.shape[1]
    begin = 0
    for left, right in zip(lefts, rights):
        steps = right[1]

        @pl.when(step == begin)
        def _(left=left):
            turned[...] = left[...].T

        @pl.when((step >= begin) & (step < begin + steps))
        def _(right=right[0]):
            product[...] = dot_plain(turned[...], right[...])

        begin += steps
    for slot in range(4):
        for out, place in ((send_ref, 4 + slot), (keep_ref, slot)):
            start = pl.multiple_of(order[place] * depth, depth)
            out[slot] = product[pl.ds(start, depth), :].astype(BF16)


def rows_terms(pairs, order):
    tokens, width = pairs[0][0].shape
    counts = [right.shape[1] // width for _, right in pairs]
    total = sum(counts)

    def right_spec(begin, count):
        return pl.BlockSpec(
            (tokens, width), lambda i, *_: (0, jnp.clip(i - begin, 0, count - 1))
        )

    begins = [sum(counts[:i]) for i in range(len(counts))]
    whole = pl.BlockSpec((tokens, width), lambda i, *_: (0, 0))
    slots = pl.BlockSpec((4, width // 8, width), lambda i, *_: (0, 0, i))

    def kernel(order_ref, *refs):
        n = len(pairs)
        rights = tuple(zip(refs[n : 2 * n], counts))
        rows_terms_kernel(n, order_ref, *refs[:n], *rights, *refs[2 * n :])

    return pl.pallas_call(
        kernel,
        grid_spec=pltpu.PrefetchScalarGridSpec(
            num_scalar_prefetch=1,
            grid=(total,),
            in_specs=[whole for _ in pairs] + [right_spec(b, c) for b, c in zip(begins, counts)],
            out_specs=[slots, slots],
            scratch_shapes=[pltpu.VMEM((width, tokens), BF16), pltpu.VMEM((width, width), F32)],
        ),
        out_shape=(jax.ShapeDtypeStruct((4, width // 8, total * width), BF16),) * 2,
        compiler_params=pltpu.CompilerParams(vmem_limit_bytes=48 << 20),
        cost_estimate=pl.CostEstimate(
            flops=2 * tokens * width * width * total,
            bytes_accessed=2 * (tokens + width) * width * total,
            transcendentals=0,
        ),
        name="rows_terms",
    )(order, *[left for left, _ in pairs], *[right for _, right in pairs])


def columns_term_kernel(order, left, right, out):
    out[0] = dot_rows(left[...], right[...]).astype(BF16)


def columns_term(left, right, order):
    tokens, width = right.shape
    depth = left.shape[1] // 8
    return pl.pallas_call(
        columns_term_kernel,
        grid_spec=pltpu.PrefetchScalarGridSpec(
            num_scalar_prefetch=1,
            grid=(4,),
            in_specs=[
                pl.BlockSpec((tokens, depth), lambda i, order: (0, order[i])),
                pl.BlockSpec((tokens, width), lambda i, order: (0, 0)),
            ],
            out_specs=pl.BlockSpec((1, depth, width), lambda i, order: (i, 0, 0)),
        ),
        out_shape=jax.ShapeDtypeStruct((4, depth, width), BF16),
        compiler_params=pltpu.CompilerParams(vmem_limit_bytes=48 << 20),
        cost_estimate=pl.CostEstimate(
            flops=2 * tokens * width * depth * 4,
            bytes_accessed=2 * (tokens * depth * 4 + tokens * width + depth * width * 4),
            transcendentals=0,
        ),
        name="columns_term",
    )(order, left, right)


class SlotMoves:
    def __init__(self):
        self.keep, self.away = slot_orders()
        self.order = jnp.concatenate([self.keep, self.away])

    def gather(self, weights, output_weight, inner_weight, outer_weight):
        depth, width = output_weight.shape
        self.columns = inner_weight.shape[1] // width
        pieces = line_gather(jnp.concatenate(weights, axis=1))
        split = [
            inner_weight[:, i * width : (i + 1) * width] for i in range(self.columns)
        ]
        self.dense_line = line_gather(jnp.concatenate([output_weight, *split]))
        lined = line_order(pieces)
        rows = lined.shape[1]
        lined = lined.reshape(4, rows, 3, -1).transpose(1, 2, 0, 3).reshape(rows, -1)
        ones = plane_gather(lined)
        two = plane_rest(ones)
        self.dense_line = behind(self.dense_line, ones)
        mine = (lined,) + ones + (two,)
        self.packed_pieces = mine + core_gather(mine)
        outer_weight = after(outer_weight, pieces[3])
        self.outer_full = lax.all_gather(outer_weight, ("rows", "heads"), axis=0, tiled=True)

    def project(self, tokens, bias):
        lined = line_order(self.dense_line)
        width = lined.shape[2]
        lined = lined.reshape(4, self.columns + 1, -1, width).transpose(1, 0, 2, 3)
        lined = lined.reshape(-1, width)
        tokens = after(tokens, lined)
        packed, full = project(self.order, tokens, bias.reshape(1, -1), self.packed_pieces)
        ones = behind(plane_gather(lined), (packed,))
        self.dense_mine = (lined,) + ones
        self.dense_depth = lined.shape[0] // (self.columns + 1)
        return after(packed, *ones), full.reshape(-1, full.shape[2])

    def dense_start(self, packed, earlier):
        mine = self.dense_mine
        got = core_gather(mine) + (plane_rest(mine[1:]),)
        got = got if earlier is None else behind(got, (earlier[0],))
        self.dense_got = got
        return after(packed, got[3])

    def dense(self, context):
        got = self.dense_got
        (last,) = behind(core_gather(got[3:]), (context,))
        pieces = self.dense_mine + got[3:] + got[:3] + (last,)
        fulls = join(self.order, pieces, self.dense_depth, self.columns)
        return tuple(full.reshape(-1, full.shape[2]) for full in fulls) + (self.outer_full,)

    def outer_terms(self, hidden_low, branch_grad):
        send = columns_term(hidden_low, branch_grad, self.away)
        keep = columns_term(after(hidden_low, send), branch_grad, self.keep)
        return keep, self.begin(scatter_steps(send, keep, stack_rows))

    def inner_terms(self, inner_pair, output_pair):
        terms = rows_terms((inner_pair, output_pair), self.order)
        return terms[1], self.begin(scatter_steps(*terms, stack_rows))

    def inner_cut(self, both):
        cut = self.columns * both.shape[1] // (self.columns + 1)
        return both[:, :cut], both[:, cut:]

    def packed_terms(self, tokens, packed_grad):
        terms = rows_terms(((tokens, packed_grad),), self.order)
        return self.begin(scatter_steps(*terms, stack_columns))

    def begin(self, steps):
        next(steps)
        return steps

    def packed_cut(self, total):
        width = total.shape[1] // 3
        return tuple(total[:, i * width : (i + 1) * width] for i in range(3))

    def behind(self, value, steps, *gates):
        return after(value, steps.send(gates))

    def hold(self, value, gate):
        return after(value, gate)

    def finish(self, steps, *gates):
        return steps.send(gates)

    def last(self, value, steps, small, earlier):
        low = steps.send(())
        totals = total_steps(after(small, low))
        value = value(low)
        done = earlier.send((value,))
        gates = (value,)
        while True:
            beside = next(totals)
            try:
                sent = steps.send((beside,) + gates)
            except StopIteration:
                return value, sent, beside, done
            gates = ()


class PlainMoves:
    def gather(self, weights, *dense):
        full = [
            lax.all_gather(lax.all_gather(w, "rows", axis=0, tiled=True), "heads", axis=1, tiled=True)
            for w in weights
        ]
        self.packed_weight = jnp.concatenate(full, axis=1)
        self.fulls = tuple(
            lax.all_gather(w, ("rows", "heads"), axis=0, tiled=True) for w in dense
        )

    def project(self, tokens, bias):
        packed = (dot_plain(tokens, self.packed_weight) + bias).astype(BF16)
        return packed, self.packed_weight

    def dense_start(self, packed, earlier):
        return packed

    def dense(self, context):
        return self.fulls

    def scatter(self, term):
        return lax.psum_scatter(term, ("rows", "heads"), scatter_dimension=0, tiled=True)

    def outer_terms(self, hidden_low, branch_grad):
        return None, self.scatter(dot_rows(hidden_low, branch_grad))

    def inner_terms(self, inner_pair, output_pair):
        both = self.scatter(dot_rows(*inner_pair)), self.scatter(dot_rows(*output_pair))
        return None, both

    def inner_cut(self, both):
        return both

    def packed_terms(self, tokens, packed_grad):
        term = dot_rows(tokens, packed_grad)
        width = tokens.shape[1]
        parts = [term[:, i * width : (i + 1) * width] for i in range(3)]
        parts = [lax.psum_scatter(p, "heads", scatter_dimension=1, tiled=True) for p in parts]
        return tuple(
            lax.psum_scatter(p, "rows", scatter_dimension=0, tiled=True) for p in parts
        )

    def packed_cut(self, total):
        return total

    def behind(self, value, steps, *gates):
        return value

    def hold(self, value, gate):
        return value

    def finish(self, steps, *gates):
        return steps

    def last(self, value, steps, small, earlier):
        return value(small), steps, lax.psum(small, ("rows", "heads")), earlier


def head_only(value, which):
    lanes = lax.broadcasted_iota(jnp.int32, value.shape, 1)
    keep = (lanes < HEAD_DIM) if which == 0 else (lanes >= HEAD_DIM)
    return jnp.where(keep, value, jnp.zeros_like(value))


def dot_lanes(left, right):
    return lax.dot_general(left, right, (((1,), (1,)), ((), ())), preferred_element_type=F32)


def dot_rows(left, right):
    return lax.dot_general(left, right, (((0,), (0,)), ((), ())), preferred_element_type=F32)


def dot_plain(left, right):
    return lax.dot_general(left, right, (((1,), (0,)), ((), ())), preferred_element_type=F32)


def forward_span(query_ref, key_ref, value_ref, context_ref, total_ref, start, length):
    span = pl.ds(start, length)
    query = query_ref[span, :] * jnp.asarray(SCALE, BF16)
    key, value = key_ref[span, :], value_ref[span, :]
    flipped = None
    for which in range(2):
        scores = dot_lanes(key, head_only(query, which))
        largest = jnp.max(scores, axis=0, keepdims=True)
        powers = jnp.exp(scores - largest)
        denominator = jnp.sum(powers, axis=0, keepdims=True)
        total_ref[0, 0, which : which + 1, span] = largest + jnp.log(denominator)
        part = dot_rows(head_only(value, which), powers.astype(BF16)) / denominator
        flipped = part if flipped is None else flipped + part
    context_ref[span, :] = flipped.T.astype(BF16)


def backward_span(
    query_ref, key_ref, value_ref, context_ref, grad_ref, total_ref, outs, start, length
):
    query_out, key_out, value_out = outs
    span = pl.ds(start, length)
    query = query_ref[span, :] * jnp.asarray(SCALE, BF16)
    key, value, grad = key_ref[span, :], value_ref[span, :], grad_ref[span, :]
    product = grad.astype(F32) * context_ref[span, :].astype(F32)
    flipped, key_sum, value_sum = None, None, None
    for which in range(2):
        query_one = head_only(query, which)
        grad_one = head_only(grad, which)
        ones = head_only(jnp.ones((8, 2 * HEAD_DIM), F32), which)
        row_dot = lax.dot_general(
            ones,
            product,
            (((1,), (1,)), ((), ())),
            precision=lax.Precision.HIGHEST,
            preferred_element_type=F32,
        )[:1]
        scores = dot_lanes(key, query_one)
        attention = jnp.exp(scores - total_ref[0, 0, which : which + 1, span])
        weight_grad = dot_lanes(value, grad_one)
        score_grad = (attention * (weight_grad - row_dot)).astype(BF16)
        value_part = dot_plain(attention.astype(BF16), grad_one)
        key_part = dot_plain(score_grad, query_one)
        query_part = dot_rows(head_only(key, which), score_grad)
        flipped = query_part if flipped is None else flipped + query_part
        key_sum = key_part if key_sum is None else key_sum + key_part
        value_sum = value_part if value_sum is None else value_sum + value_part
    query_out[span, :] = (flipped.T * SCALE).astype(BF16)
    key_out[span, :] = key_sum.astype(BF16)
    value_out[span, :] = value_sum.astype(BF16)


def by_kind(kind, run):
    @pl.when(kind != 1)
    def _():
        run(0, BLOCK)

    @pl.when(kind == 1)
    def _():
        length = BLOCK // PARTS

        @pl.loop(0, PARTS)
        def _(part):
            run(pl.multiple_of(part * length, length), length)


def forward_kernel(block, kinds, query_ref, key_ref, value_ref, *refs):
    def run(start, length):
        forward_span(query_ref, key_ref, value_ref, *refs[-2:], start, length)

    by_kind(kinds[block], run)


def backward_kernel(block, kinds, *refs):
    def run(start, length):
        backward_span(*refs[:6], refs[-3:], start, length)

    by_kind(kinds[block], run)


def attend(kernel, block, kinds, operands, earlier, outs, cost, name):
    pairs = outs[0].shape[1] // (2 * HEAD_DIM)

    def spec(offset):
        if offset is None:
            return pl.BlockSpec((1, 1, 2, BLOCK), lambda p, *_: (block, p, 0, 0))
        return pl.BlockSpec((BLOCK, 2 * HEAD_DIM), lambda p, *_: (block, p + offset))

    given = () if earlier is None else earlier
    first = 1 + len(operands)
    return pl.pallas_call(
        functools.partial(kernel, block),
        grid_spec=pltpu.PrefetchScalarGridSpec(
            num_scalar_prefetch=1,
            grid=(pairs,),
            in_specs=[spec(offset) for _, offset in operands] + [HBM for _ in given],
            out_specs=[spec(None if len(out.shape) == 4 else 0) for out in outs],
        ),
        out_shape=outs,
        input_output_aliases={first + i: i for i in range(len(given))},
        cost_estimate=cost,
        name=name,
    )(kinds, *[operand for operand, _ in operands], *given)


def attend_forward(block, kinds, packed, earlier):
    tokens, width = packed.shape[0], packed.shape[1] // 3
    pairs = width // (2 * HEAD_DIM)
    outs = (
        jax.ShapeDtypeStruct((tokens, width), BF16),
        jax.ShapeDtypeStruct((tokens // BLOCK, pairs, 2, BLOCK), F32),
    )
    cost = pl.CostEstimate(
        flops=16 * BLOCK * BLOCK * width,
        bytes_accessed=8 * BLOCK * width,
        transcendentals=BLOCK * BLOCK * width // HEAD_DIM,
    )
    operands = [(packed, 0), (packed, pairs), (packed, 2 * pairs)]
    return attend(forward_kernel, block, kinds, operands, earlier, outs, cost, "attend_forward")


def attend_backward(block, kinds, packed, context, context_grad, totals, earlier):
    tokens, width = context.shape
    pairs = width // (2 * HEAD_DIM)
    outs = (jax.ShapeDtypeStruct((tokens, width), BF16),) * 3
    cost = pl.CostEstimate(
        flops=40 * BLOCK * BLOCK * width,
        bytes_accessed=16 * BLOCK * width,
        transcendentals=BLOCK * BLOCK * width // HEAD_DIM,
    )
    operands = [(packed, 0), (packed, pairs), (packed, 2 * pairs), (context, 0)]
    operands += [(context_grad, 0), (totals, None)]
    return attend(backward_kernel, block, kinds, operands, earlier, outs, cost, "attend_backward")


def gelu_exact(inner):
    return 0.5 * inner * (1.0 + lax.erf(inner * 0.7071067811865476))


def norm_apply(hidden_in, norm_gain, norm_shift):
    average = jnp.mean(hidden_in, axis=-1, keepdims=True)
    centred = hidden_in - average
    variance = jnp.mean(centred * centred, axis=-1, keepdims=True)
    return centred * lax.rsqrt(variance + EPSILON) * norm_gain + norm_shift


def shards(
    tokens,
    block_kind,
    query_weight,
    key_weight,
    value_weight,
    query_bias,
    value_bias,
    output_weight,
    output_bias,
    first_gain,
    first_shift,
    inner_weight,
    inner_bias,
    outer_weight,
    outer_bias,
    second_gain,
    second_shift,
    cotangent,
):
    width = tokens.shape[1]
    per_device = block_kind.shape[0] // lax.axis_size("heads")
    kinds = lax.dynamic_slice_in_dim(
        block_kind, lax.axis_index("heads") * per_device, per_device
    )
    valid = jnp.repeat((kinds != 2).astype(F32), BLOCK)[:, None]

    eight_by_four = lax.axis_size("rows") == 8 and lax.axis_size("heads") == 4
    moves = SlotMoves() if eight_by_four else PlainMoves()
    moves.gather(
        (query_weight, key_weight, value_weight), output_weight, inner_weight, outer_weight
    )

    packed_bias = jnp.concatenate([query_bias, jnp.zeros_like(query_bias), value_bias])
    packed, packed_weight = moves.project(tokens, packed_bias.astype(F32))
    earlier = None
    for block in range(per_device):
        if block == per_device - 1:
            packed = moves.dense_start(packed, earlier)
        earlier = attend_forward(block, kinds, packed, earlier)
    context, totals = earlier
    output_full, inner_full, outer_full = moves.dense(context)

    attended = dot_plain(context, output_full) + output_bias
    first_sum = tokens.astype(F32) + attended
    first_out = norm_apply(first_sum, first_gain, first_shift)
    first_low = first_out.astype(BF16)
    inner_pre = dot_plain(first_low, inner_full) + inner_bias
    hidden_low = gelu_exact(inner_pre).astype(BF16)
    second_sum = first_out + (dot_plain(hidden_low, outer_full) + outer_bias)
    final = norm_apply(second_sum, second_gain, second_shift)
    layer_out = (final * valid).astype(BF16)

    out_grad = cotangent.astype(F32) * valid
    _, second_pull = jax.vjp(
        norm_apply, second_sum, second_gain.astype(F32), second_shift.astype(F32)
    )
    second_grad, second_gain_grad, second_shift_grad = second_pull(out_grad)
    branch_grad = second_grad.astype(BF16)
    kernel_done, outer_steps = moves.outer_terms(hidden_low, branch_grad)
    outer_bias_grad = jnp.sum(branch_grad, axis=0, dtype=F32)
    branch_grad = moves.behind(branch_grad, outer_steps, kernel_done)
    hidden_grad = dot_lanes(branch_grad, outer_full)
    _, gelu_pull = jax.vjp(gelu_exact, inner_pre)
    inner_grad = gelu_pull(hidden_grad)[0].astype(BF16)
    inner_bias_grad = jnp.sum(inner_grad, axis=0, dtype=F32)
    inner_grad = moves.behind(inner_grad, outer_steps, inner_grad)
    first_out_grad = second_grad + dot_lanes(inner_grad, inner_full)
    _, first_pull = jax.vjp(
        norm_apply, first_sum, first_gain.astype(F32), first_shift.astype(F32)
    )
    first_grad, first_gain_grad, first_shift_grad = first_pull(first_out_grad)
    attended_grad = first_grad.astype(BF16)
    output_bias_grad = jnp.sum(attended_grad, axis=0, dtype=F32)
    terms_grad = moves.behind(attended_grad, outer_steps, attended_grad)
    kernel_done, inner_steps = moves.inner_terms((first_low, inner_grad), (context, terms_grad))
    outer_weight_grad = moves.finish(outer_steps, kernel_done)
    attended_grad = moves.hold(attended_grad, outer_weight_grad)
    context_grad = dot_lanes(attended_grad, output_full).astype(BF16)
    context_grad = moves.behind(context_grad, inner_steps, context_grad)
    pieces = None
    for block in range(per_device):
        if block > 0:
            context_grad = moves.behind(context_grad, inner_steps, pieces[0])
        pieces = attend_backward(block, kinds, packed, context, context_grad, totals, pieces)
    packed_grad = jnp.concatenate(pieces, axis=1)
    packed_grad = moves.behind(packed_grad, inner_steps, pieces[0])
    packed_steps = moves.packed_terms(tokens, packed_grad)
    sums = (
        jnp.sum(pieces[0], axis=0, dtype=F32),
        jnp.sum(pieces[2], axis=0, dtype=F32),
        output_bias_grad,
        first_gain_grad,
        first_shift_grad,
        outer_bias_grad,
        second_gain_grad,
        second_shift_grad,
    )
    inner_rows = inner_bias_grad.reshape(-1, width)

    def tokens_part(gate):
        return first_grad + dot_lanes(after(packed_grad, gate), packed_weight)

    tokens_grad, packed_total, small, inner_both = moves.last(
        tokens_part, packed_steps, jnp.concatenate([jnp.stack(sums), inner_rows]), inner_steps
    )
    inner_weight_grad, output_weight_grad = moves.inner_cut(inner_both)
    query_weight_grad, key_weight_grad, value_weight_grad = moves.packed_cut(packed_total)
    return (
        layer_out,
        tokens_grad,
        query_weight_grad,
        key_weight_grad,
        value_weight_grad,
        small[0],
        small[1],
        output_weight_grad,
        small[2],
        small[3],
        small[4],
        inner_weight_grad,
        small[len(sums) :].reshape(-1),
        outer_weight_grad,
        small[5],
        small[6],
        small[7],
    )


def solution(mesh):
    both = P(("rows", "heads"), None)
    placed = (
        (both, P("rows"))
        + (P("rows", "heads"),) * 3
        + (P(), P(), both, P(), P(), P(), both, P(), both, P(), P(), P(), both)
    )
    given = (
        (both, both)
        + (P("rows", "heads"),) * 3
        + (P(), P(), both, P(), P(), P(), both, P(), both, P(), P(), P())
    )
    return jax.shard_map(
        shards, mesh=mesh, in_specs=placed, out_specs=given, check_vma=False
    )
```

profile of v0, /device:TPU:0, one launch (start us, length us, event | category | flops | bytes accessed | tf_op | source)
XLA Modules:
  0.0 365.1 jit_solution(7513418212634838161)
XLA Ops:
  10.1 5.1 %collective-permute-start.3 = (bf16[96,576]{0,1:T(8,128)(2,1)S(1)}, bf16[96,576]{0,1:T(8,128)(2,1)S(1)}, u32[]{:S(2)}, u32[]{:S(2)}) collective-permute-start(bf16[96,576]{0,1:T(8,128)(2,1)S(1)} %pad_maximum_fusion.2), channel_id=1, source_target_pairs={{0,3},{1,0},{2,1},{3,2},{4,7},{5,4},{6,5},{7,6},{8,11},{9,8},{10,9... | collective-permute-start | bytes 331784 | tf_op jit(solution)/shard_map/ppermute | solution.py:32
  15.2 3.4 collective-permute-done.3
  18.8 4.7 %collective-permute-start.4 = (bf16[96,576]{0,1:T(8,128)(2,1)S(1)}, bf16[96,576]{0,1:T(8,128)(2,1)S(1)}, u32[]{:S(2)}, u32[]{:S(2)}) collective-permute-start(bf16[96,576]{0,1:T(8,128)(2,1)S(1)} %pad_maximum_fusion.2), channel_id=1, source_target_pairs={{0,2},{1,3},{2,0},{3,1},{4,6},{5,7},{6,4},{7,5},{8,10},{9,11},{10,... | collective-permute-start | bytes 331784 | tf_op jit(solution)/shard_map/ppermute | solution.py:32
  25.8 1.5 collective-permute-done.5
  27.3 4.6 %collective-permute-done.4 = bf16[96,576]{0,1:T(8,128)(2,1)S(1)} collective-permute-done((bf16[96,576]{0,1:T(8,128)(2,1)S(1)}, bf16[96,576]{0,1:T(8,128)(2,1)S(1)}, u32[]{:S(2)}, u32[]{:S(2)}) %collective-permute-start.4) | collective-permute-done | bytes 110624 | tf_op jit(solution)/shard_map/ppermute | solution.py:32
  33.6 1.6 collective-permute-start.7
  35.2 1.5 collective-permute-start.6
  37.0 1.8 collective-permute-start
  38.8 7.7 %collective-permute-done.7.refs_2_ = bf16[96,2304]{1,0:T(8,128)(2,1)S(1)} collective-permute-done((bf16[96,2304]{1,0:T(8,128)(2,1)S(1)}, bf16[96,2304]{1,0:T(8,128)(2,1)S(1)}, u32[]{:S(2)}, u32[]{:S(2)}) %collective-permute-start.7) | collective-permute-done | bytes 442400 | tf_op jit(solution)/shard_map/ppermute | solution.py:28
  46.4 1.6 collective-permute-start.8
  48.0 6.3 %collective-permute-done.1 = bf16[120,768]{1,0:T(8,128)(2,1)S(1)} collective-permute-done((bf16[120,768]{1,0:T(8,128)(2,1)S(1)}, bf16[120,768]{1,0:T(8,128)(2,1)S(1)}, u32[]{:S(2)}, u32[]{:S(2)}) %collective-permute-start.1) | collective-permute-done | bytes 184352 | tf_op jit(solution)/shard_map/ppermute | solution.py:32
  56.8 1.6 collective-permute-done.11.refs_6_
  60.4 10.4 %project.1 = (bf16[1024,2304]{1,0:T(8,128)(2,1)}, bf16[8,96,2304]{2,1,0:T(8,128)(2,1)}) custom-call(s32[8]{0:T(128)S(1)} %concatenate.32.order.order_ref, bf16[1024,768]{1,0:T(8,128)(2,1)} %refs_0_.1, f32[1,2304]{1,0:T(1,128)S(1)} %fusion.10.bias, bf16[96,2304]{1,0:T(8,128)(2,1)S(1)} %reshape.237.refs_0_, bf16[96,2304]{1,0:T(8,128)(2,1)} %collective-permute-done.6.refs_1_, ...), custom_call_target="tpu_custom_call" | custom-call | flops 3623878656 | bytes 13369344 | tf_op jit(solution)/shard_map/project/pallas_call | solution.py:152
  70.8 3.0 collective-permute-done.14.refs_2_
  73.8 2.1 collective-permute-done.13.refs_1_
  78.2 17.7 %attend_forward.2 = (bf16[1024,768]{1,0:T(8,128)(2,1)}, f32[2,6,2,512]{3,2,1,0:T(2,128)}) custom-call(s32[2]{0:T(128)} %get-tuple-element.181.kinds, bf16[1024,2304]{1,0:T(8,128)(2,1)} %get-tuple-element.92.query_ref.key_ref.value_ref.refs_0_.refs_1_.refs_2_, bf16[1024,2304]{1,0:T(8,128)(2,1)} %get-tuple-element.92.query_ref.key_ref.value_ref.refs_0_.refs_1_.refs_2_, ...), custom_call_target="tpu_custom_call" | custom-call | flops 3221225472 | bytes 3145728 | tf_op jit(solution)/shard_map/attend_forward/pallas_call | solution.py:568
  96.2 10.8 %attend_forward.3 = (bf16[1024,768]{1,0:T(8,128)(2,1)}, f32[2,6,2,512]{3,2,1,0:T(2,128)}) custom-call(s32[2]{0:T(128)} %get-tuple-element.181.kinds, bf16[1024,2304]{1,0:T(8,128)(2,1)} %get-tuple-element.92.query_ref.key_ref.value_ref.refs_0_.refs_1_.refs_2_, ...), custom_call_target="tpu_custom_call", output_to_operand_aliasing={{0}: (4, {}), {1}: (5, {})} | custom-call | flops 3221225472 | bytes 3145728 | tf_op jit(solution)/shard_map/attend_forward/pallas_call | solution.py:568
  107.0 6.1 %join.1 = (bf16[8,96,768]{2,1,0:T(8,128)(2,1)}, bf16[8,96,3072]{2,1,0:T(8,128)(2,1)}) custom-call(s32[8]{0:T(128)S(1)} %concatenate.32.order.order_ref, bf16[480,768]{1,0:T(8,128)(2,1)S(1)} %bitcast.98, bf16[480,768]{1,0:T(8,128)(2,1)S(1)} %collective-permute-done.13.refs_1_, bf16[480,768]{1,0:T(8,128)(2,1)S(1)} %collective-permute-done.14.refs_2_, ...), custom_call_target="tpu_custom_call" | custom-call | bytes 11796480 | tf_op jit(solution)/shard_map/join/pallas_call | solution.py:199
  113.1 2.8 fusion.16
  118.2 1.2 copy-done.36
  119.4 9.8 %multiply_convert_fusion = (bf16[1024,3072]{1,0:T(8,128)(2,1)}, f32[1024,3072]{1,0:T(8,128)}) fusion(f32[3072]{0:T(1024)S(1)} %convert_element_type.264, bf16[1024,768]{1,0:T(8,128)(2,1)S(1)} %fusion.2.refs_0_, bf16[768,3072]{1,0:T(8,128)(2,1)S(1)} %bitcast.115), kind=kOutput, calls=%fused_computation.2 | convolution fusion | flops 4850712576 | bytes 25178112 | tf_op jit(solution)/shard_map/dot_general | solution.py:476
  129.2 9.3 %fusion.17 = (f32[1024]{0:T(1024)S(1)}, f32[1024,768]{1,0:T(8,128)S(1)}) fusion(f32[768]{0:T(1024)S(1)} %convert_element_type.266, bf16[1024,3072]{1,0:T(8,128)(2,1)} %get-tuple-element.102.left, bf16[3072,768]{1,0:T(8,128)(2,1)} %all-gather.2.cloned.1.call-done, f32[768]{0:T(1024)S(1)} %convert_element_type.262, f32[768]{0:T(1024)S(1)} %convert_element_type.261, ...), kind=kOutput, calls=%fused_computation.111 | convolution fusion | flops 4837342208 | bytes 17323008 | tf_op jit(solution)/shard_map/dot_general | solution.py:476
  139.9 2.3 multiply_reduce_fusion
  142.2 3.2 fusion.14
  145.4 1.6 copy-done.8
  147.4 6.4 %columns_term.2 = bf16[4,384,768]{2,1,0:T(8,128)(2,1)} custom-call(s32[4]{0:T(128)S(1)} %add_xor_fusion.order, bf16[1024,3072]{1,0:T(8,128)(2,1)} %get-tuple-element.102.left, bf16[1024,768]{1,0:T(8,128)(2,1)S(1)} %get-tuple-element.104.right), custom_call_target="tpu_custom_call" | custom-call | flops 2415919104 | bytes 7077888 | tf_op jit(solution)/shard_map/columns_term/pallas_call | solution.py:281
  153.8 7.3 %collective-permute-start.20 = (bf16[4,384,768]{2,1,0:T(8,128)(2,1)}, bf16[4,384,768]{2,1,0:T(8,128)(2,1)}, u32[]{:S(2)}, u32[]{:S(2)}) collective-permute-start(bf16[4,384,768]{2,1,0:T(8,128)(2,1)} %columns_term.2), channel_id=1, source_target_pairs={{0,4},{4,0},{8,12},{12,8},{16,20},{20,16},{24,28},{28,24},{1,5},{5... | collective-permute-start | bytes 7077896 | tf_op jit(solution)/shard_map/ppermute | solution.py:28
  161.2 5.4 %columns_term.3 = bf16[4,384,768]{2,1,0:T(8,128)(2,1)S(1)} custom-call(s32[4]{0:T(128)S(1)} %add_add_fusion.7.order, bf16[1024,3072]{1,0:T(8,128)(2,1)} %get-tuple-element.102.left, bf16[1024,768]{1,0:T(8,128)(2,1)S(1)} %get-tuple-element.104.right), custom_call_target="tpu_custom_call" | custom-call | flops 2415919104 | bytes 7077888 | tf_op jit(solution)/shard_map/columns_term/pallas_call | solution.py:281
  166.6 1.7 add_convert_fusion.4
  168.5 15.0 %convert_reduce_fusion = (f32[3072]{0:T(1024)}, bf16[1024,3072]{1,0:T(8,128)(2,1)}) fusion(bf16[1024,768]{1,0:T(8,128)(2,1)S(1)} %get-tuple-element.104.right, bf16[3072,768]{1,0:T(8,128)(2,1)} %all-gather.2.cloned.1.call-done, f32[1024,3072]{1,0:T(8,128)} %get-tuple-element.206, f32[3072]{0:T(1024)S(1)} %convert_element_type.264), kind=kOutput, calls=%fused_computation | convolution fusion | flops 4882166784 | bytes 25190400 | tf_op jit(solution)/shard_map/dot_general | solution.py:468
  184.6 1.3 fusion.7
  186.6 8.9 %multiply_reduce_fusion.1 = (f32[768]{0:T(1024)}, f32[1024]{0:T(1024)S(1)}, f32[768]{0:T(1024)}, f32[1024,768]{1,0:T(8,128)S(1)}) fusion(f32[1024,768]{1,0:T(8,128)S(1)} %copy-done.7, f32[1024]{0:T(1024)S(1)} %fusion.11, f32[1024]{0:T(1024)S(1)} %broadcast_multiply_fusion.1, f32[768]{0:T(1024)S(1)} %convert_element_type.261, ...), kind=kOutput, calls=%fused_computation.9 | convolution fusion | flops 4839699456 | bytes 20472832 | tf_op jit(solution)/shard_map/dot_general | solution.py:468
  195.5 1.5 fusion.13
  197.4 2.6 fusion.4
  201.6 12.0 %rows_terms.2 = (bf16[4,96,3840]{2,1,0:T(8,128)(2,1)}, bf16[4,96,3840]{2,1,0:T(8,128)(2,1)}) custom-call(s32[8]{0:T(128)S(1)} %concatenate.32.order.order_ref, bf16[1024,768]{1,0:T(8,128)(2,1)S(1)} %fusion.2.refs_0_, bf16[1024,768]{1,0:T(8,128)(2,1)S(1)} %copy-done.1, bf16[1024,3072]{1,0:T(8,128)(2,1)} %get-tuple-element.106.refs_2_, ...), custom_call_target="tpu_custom_call" | custom-call | flops 6039797760 | bytes 13762560 | tf_op jit(solution)/shard_map/rows_terms/pallas_call | solution.py:254
  214.9 2.7 collective-permute-start.25
  217.5 10.2 %collective-permute-done.24 = bf16[96,768]{1,0:T(8,128)(2,1)S(1)} collective-permute-done((bf16[96,768]{1,0:T(8,128)(2,1)}, bf16[96,768]{1,0:T(8,128)(2,1)S(1)}, u32[]{:S(2)}, u32[]{:S(2)}) %collective-permute-start.24) | collective-permute-done | bytes 147488 | tf_op jit(solution)/shard_map/ppermute | solution.py:32
  227.7 1.7 convert_add_fusion.2
  229.4 4.0 %convolution_convert_fusion.refs_4_ = bf16[1024,768]{1,0:T(8,128)(2,1)} fusion(bf16[1024,768]{1,0:T(8,128)(2,1)S(1)} %get-tuple-element.113.refs_3_, bf16[768,768]{1,0:T(8,128)(2,1)} %bitcast.120), kind=kOutput, calls=%fused_computation.32 | convolution fusion | flops 1208745984 | bytes 4325376 | tf_op jit(solution)/shard_map/dot_general | solution.py:468
  233.5 2.9 add_convert_fusion.3
  237.1 19.1 %attend_backward.2 = (bf16[1024,768]{1,0:T(8,128)(2,1)}, bf16[1024,768]{1,0:T(8,128)(2,1)}, bf16[1024,768]{1,0:T(8,128)(2,1)}) custom-call(s32[2]{0:T(128)} %get-tuple-element.181.kinds, bf16[1024,2304]{1,0:T(8,128)(2,1)} %get-tuple-element.92.query_ref.key_ref.value_ref.refs_0_.refs_1_.refs_2_, ...), custom_call_target="tpu_custom_call" | custom-call | flops 8053063680 | bytes 6291456 | tf_op jit(solution)/shard_map/attend_backward/pallas_call | solution.py:568
  256.3 2.5 fusion.6
  258.8 1.5 collective-permute-start.28
  260.2 14.1 %attend_backward.3 = (bf16[1024,768]{1,0:T(8,128)(2,1)}, bf16[1024,768]{1,0:T(8,128)(2,1)}, bf16[1024,768]{1,0:T(8,128)(2,1)}) custom-call(s32[2]{0:T(128)} %get-tuple-element.181.kinds, bf16[1024,2304]{1,0:T(8,128)(2,1)} %get-tuple-element.92.query_ref.key_ref.value_ref.refs_0_.refs_1_.refs_2_, ...), custom_call_target="tpu_custom_call", output_to_operand_aliasing={{0}: (7, {}), {1}: (8, {}), {2}: (9, {})} | custom-call | flops 8053063680 | bytes 6291456 | tf_op jit(solution)/shard_map/attend_backward/pallas_call | solution.py:568
  274.3 3.9 %pad_maximum_fusion.refs_1_ = bf16[1024,2304]{1,0:T(8,128)(2,1)} fusion(bf16[1024,768]{1,0:T(8,128)(2,1)} %get-tuple-element.125, bf16[1024,768]{1,0:T(8,128)(2,1)} %get-tuple-element.124, bf16[1024,768]{1,0:T(8,128)(2,1)} %get-tuple-element.123), kind=kLoop, calls=%fused_computation.6 | loop fusion | flops 14155776 | bytes 9437184 | tf_op jit(solution)/shard_map/concatenate | solution.py:709
  278.2 2.0 fusion.3
  281.4 7.9 %rows_terms.3 = (bf16[4,96,2304]{2,1,0:T(8,128)(2,1)}, bf16[4,96,2304]{2,1,0:T(8,128)(2,1)S(1)}) custom-call(s32[8]{0:T(128)S(1)} %concatenate.32.order.order_ref, bf16[1024,768]{1,0:T(8,128)(2,1)S(1)} %copy-done.3, bf16[1024,2304]{1,0:T(8,128)(2,1)} %pad_maximum_fusion.refs_1_), custom_call_target="tpu_custom_call" | custom-call | flops 3623878656 | bytes 8257536 | tf_op jit(solution)/shard_map/rows_terms/pallas_call | solution.py:254
  289.3 3.6 collective-permute-start.29
  294.8 1.3 reshape.244
  296.1 1.3 reshape.245
  297.9 1.9 convert_reduce_fusion.3
  300.7 1.4 add_convert_fusion.5
  303.5 6.4 %collective-permute-start.42 = (bf16[24,3840]{1,0:T(8,128)(2,1)}, bf16[24,3840]{1,0:T(8,128)(2,1)S(1)}, u32[]{:S(2)}, u32[]{:S(2)}) collective-permute-start(bf16[24,3840]{1,0:T(8,128)(2,1)} %get-tuple-element.183), channel_id=1, source_target_pairs={{0,2},{1,3},{2,0},{3,1},{4,6},{5,7},{6,4},{7,5},{8,10},{9,11},{10,... | collective-permute-start | bytes 552968 | tf_op jit(solution)/shard_map/ppermute | solution.py:32
  309.9 1.4 collective-permute-start.30
  312.2 9.8 %add_add_fusion.4 = f32[1024,768]{1,0:T(8,128)} fusion(f32[1024,768]{1,0:T(8,128)} %copy-done.10, bf16[1024,2304]{1,0:T(8,128)(2,1)} %pad_maximum_fusion.refs_1_, bf16[768,2304]{1,0:T(8,128)(2,1)} %bitcast.121, f32[1024]{0:T(1024)S(1)} %copy-done.21), kind=kOutput, calls=%fused_computation.24 | convolution fusion | flops 3625451520 | bytes 14553088 | tf_op jit(solution)/shard_map/dot_general | solution.py:468
  322.0 4.6 %collective-permute-done.42 = bf16[24,3840]{1,0:T(8,128)(2,1)S(1)} collective-permute-done((bf16[24,3840]{1,0:T(8,128)(2,1)}, bf16[24,3840]{1,0:T(8,128)(2,1)S(1)}, u32[]{:S(2)}, u32[]{:S(2)}) %collective-permute-start.42) | collective-permute-done | bytes 184352 | tf_op jit(solution)/shard_map/ppermute | solution.py:32
  326.8 1.9 collective-permute-start.38
  329.9 1.2 collective-permute-start.32
  334.9 3.3 collective-permute-done.32
  338.2 1.2 fusion.5
  340.9 2.4 collective-permute-start.36
  344.0 1.9 collective-permute-start.34
  345.9 1.8 slice_reduce_fusion
  347.7 8.0 %collective-permute-done.35 = bf16[96,576]{0,1:T(8,128)(2,1)S(1)} collective-permute-done((bf16[96,576]{0,1:T(8,128)(2,1)S(1)}, bf16[96,576]{0,1:T(8,128)(2,1)S(1)}, u32[]{:S(2)}, u32[]{:S(2)}) %collective-permute-start.35) | collective-permute-done | bytes 110624 | tf_op jit(solution)/shard_map/ppermute | solution.py:32
  (214 shorter events, 40.1 us)
Async XLA Ops:
  7.2 29.5 %copy-start.19 = (bf16[24,3072]{1,0:T(8,128)(2,1)S(1)}, bf16[24,3072]{1,0:T(8,128)(2,1)}, u32[]{:S(2)}) copy-start(bf16[24,3072]{1,0:T(8,128)(2,1)} %param.29) | copy-start | bytes 442372
  7.2 122.0 %all-gather.2.cloned.1.call-start = ((), (), s32[]{:S(2)}) async-start(), calls=%async_computation | async-start | bytes 4866048 | tf_op jit(solution)/shard_map/all_gather | solution.py:325
  10.1 8.5 %collective-permute-start.3 = (bf16[96,576]{0,1:T(8,128)(2,1)S(1)}, bf16[96,576]{0,1:T(8,128)(2,1)S(1)}, u32[]{:S(2)}, u32[]{:S(2)}) collective-permute-start(bf16[96,576]{0,1:T(8,128)(2,1)S(1)} %pad_maximum_fusion.2), channel_id=1, source_target_pairs={{0,3},{1,0},{2,1},{3,2},{4,7},{5,4},{6,5},{7,6},{8,11},{9,8},{10,9... | collective-permute-start | bytes 331784 | tf_op jit(solution)/shard_map/ppermute | solution.py:32
  18.6 8.7 %collective-permute-start.5 = (bf16[96,576]{0,1:T(8,128)(2,1)S(1)}, bf16[96,576]{0,1:T(8,128)(2,1)S(1)}, u32[]{:S(2)}, u32[]{:S(2)}) collective-permute-start(bf16[96,576]{0,1:T(8,128)(2,1)S(1)} %pad_maximum_fusion.2), channel_id=1, source_target_pairs={{0,1},{1,2},{2,3},{3,0},{4,5},{5,6},{6,7},{7,4},{8,9},{9,10},{10,1... | collective-permute-start | bytes 331784 | tf_op jit(solution)/shard_map/ppermute | solution.py:32
  18.8 13.1 %collective-permute-start.4 = (bf16[96,576]{0,1:T(8,128)(2,1)S(1)}, bf16[96,576]{0,1:T(8,128)(2,1)S(1)}, u32[]{:S(2)}, u32[]{:S(2)}) collective-permute-start(bf16[96,576]{0,1:T(8,128)(2,1)S(1)} %pad_maximum_fusion.2), channel_id=1, source_target_pairs={{0,2},{1,3},{2,0},{3,1},{4,6},{5,7},{6,4},{7,5},{8,10},{9,11},{10,... | collective-permute-start | bytes 331784 | tf_op jit(solution)/shard_map/ppermute | solution.py:32
  32.1 24.6 %copy-start.33 = (bf16[768]{0:T(1024)(128)(2,1)S(1)}, bf16[768]{0:T(1024)(128)(2,1)}, u32[]{:S(2)}) copy-start(bf16[768]{0:T(1024)(128)(2,1)} %param.23) | copy-start | bytes 4612
  32.1 24.6 %copy-start.34 = (bf16[768]{0:T(1024)(128)(2,1)S(1)}, bf16[768]{0:T(1024)(128)(2,1)}, u32[]{:S(2)}) copy-start(bf16[768]{0:T(1024)(128)(2,1)} %param.24) | copy-start | bytes 4612
  33.6 12.8 %collective-permute-start.7 = (bf16[96,2304]{1,0:T(8,128)(2,1)S(1)}, bf16[96,2304]{1,0:T(8,128)(2,1)S(1)}, u32[]{:S(2)}, u32[]{:S(2)}) collective-permute-start(bf16[96,2304]{1,0:T(8,128)(2,1)S(1)} %reshape.237.refs_0_), channel_id=1, source_target_pairs={{0,16},{4,12},{8,24},{12,4},{16,0},{20,28},{24,8},{28,20},{1,17},{... | collective-permute-start | bytes 1327112 | tf_op jit(solution)/shard_map/ppermute | solution.py:28
  35.2 11.3 %collective-permute-start.6 = (bf16[96,2304]{1,0:T(8,128)(2,1)S(1)}, bf16[96,2304]{1,0:T(8,128)(2,1)}, u32[]{:S(2)}, u32[]{:S(2)}) collective-permute-start(bf16[96,2304]{1,0:T(8,128)(2,1)S(1)} %reshape.237.refs_0_), channel_id=1, source_target_pairs={{0,8},{4,20},{8,0},{12,28},{16,24},{20,4},{24,16},{28,12},{1,9},{5... | collective-permute-start | bytes 1327112 | tf_op jit(solution)/shard_map/ppermute | solution.py:28
  36.7 11.4 %collective-permute-start.2 = (bf16[120,768]{1,0:T(8,128)(2,1)S(1)}, bf16[120,768]{1,0:T(8,128)(2,1)S(1)}, u32[]{:S(2)}, u32[]{:S(2)}) collective-permute-start(bf16[120,768]{1,0:T(8,128)(2,1)S(1)} %slice_dynamic-update-slice_fusion), channel_id=1, source_target_pairs={{0,3},{1,0},{2,1},{3,2},{4,7},{5,4},{6,5},{7,6},{8,11},{9,8},{10,9... | collective-permute-start | bytes 552968 | tf_op jit(solution)/shard_map/ppermute | solution.py:32
  37.0 17.3 %collective-permute-start.1 = (bf16[120,768]{1,0:T(8,128)(2,1)S(1)}, bf16[120,768]{1,0:T(8,128)(2,1)S(1)}, u32[]{:S(2)}, u32[]{:S(2)}) collective-permute-start(bf16[120,768]{1,0:T(8,128)(2,1)S(1)} %slice_dynamic-update-slice_fusion), channel_id=1, source_target_pairs={{0,2},{1,3},{2,0},{3,1},{4,6},{5,7},{6,4},{7,5},{8,10},{9,11},{10,... | collective-permute-start | bytes 552968 | tf_op jit(solution)/shard_map/ppermute | solution.py:32
  37.0 17.3 %collective-permute-start = (bf16[120,768]{1,0:T(8,128)(2,1)S(1)}, bf16[120,768]{1,0:T(8,128)(2,1)S(1)}, u32[]{:S(2)}, u32[]{:S(2)}) collective-permute-start(bf16[120,768]{1,0:T(8,128)(2,1)S(1)} %slice_dynamic-update-slice_fusion), channel_id=1, source_target_pairs={{0,1},{1,2},{2,3},{3,0},{4,5},{5,6},{6,7},{7,4},{8,9},{9,10},{10,1... | collective-permute-start | bytes 552968 | tf_op jit(solution)/shard_map/ppermute | solution.py:32
  46.4 9.5 %collective-permute-start.9 = (bf16[96,2304]{1,0:T(8,128)(2,1)S(1)}, bf16[96,2304]{1,0:T(8,128)(2,1)}, u32[]{:S(2)}, u32[]{:S(2)}) collective-permute-start(bf16[96,2304]{1,0:T(8,128)(2,1)S(1)} %reshape.237.refs_0_), channel_id=1, source_target_pairs={{0,4},{4,0},{8,12},{12,8},{16,20},{20,16},{24,28},{28,24},{1,5},{5... | collective-permute-start | bytes 1327112 | tf_op jit(solution)/shard_map/ppermute | solution.py:28
  46.4 10.0 %collective-permute-start.8 = (bf16[96,2304]{1,0:T(8,128)(2,1)}, bf16[96,2304]{1,0:T(8,128)(2,1)}, u32[]{:S(2)}, u32[]{:S(2)}) collective-permute-start(bf16[96,2304]{1,0:T(8,128)(2,1)} %collective-permute-done.6.refs_1_), channel_id=1, source_target_pairs={{0,16},{4,12},{8,24},{12,4},{16,0},{20,28},{24,8},{28,20},{1,17},{... | collective-permute-start | bytes 1327112 | tf_op jit(solution)/shard_map/ppermute | solution.py:28
  54.5 19.3 %collective-permute-start.14 = (bf16[480,768]{1,0:T(8,128)(2,1)S(1)}, bf16[480,768]{1,0:T(8,128)(2,1)S(1)}, u32[]{:S(2)}, u32[]{:S(2)}) collective-permute-start(bf16[480,768]{1,0:T(8,128)(2,1)S(1)} %bitcast.95), channel_id=1, source_target_pairs={{0,16},{4,12},{8,24},{12,4},{16,0},{20,28},{24,8},{28,20},{1,17},{... | collective-permute-start | bytes 2211848 | tf_op jit(solution)/shard_map/ppermute | solution.py:28
  55.3 20.7 %collective-permute-start.13 = (bf16[480,768]{1,0:T(8,128)(2,1)S(1)}, bf16[480,768]{1,0:T(8,128)(2,1)S(1)}, u32[]{:S(2)}, u32[]{:S(2)}) collective-permute-start(bf16[480,768]{1,0:T(8,128)(2,1)S(1)} %bitcast.96), channel_id=1, source_target_pairs={{0,8},{4,20},{8,0},{12,28},{16,24},{20,4},{24,16},{28,12},{1,9},{5... | collective-permute-start | bytes 2211848 | tf_op jit(solution)/shard_map/ppermute | solution.py:28
  55.9 2.5 collective-permute-start.11
  55.9 2.8 collective-permute-start.10
  56.5 2.9 collective-permute-start.12
  56.7 20.8 %copy-start.35 = (s32[8]{0:T(128)S(1)}, s32[8]{0:T(128)}, u32[]{:S(2)}) copy-start(s32[8]{0:T(128)} %param.19) | copy-start | bytes 100
  58.4 37.5 %collective-permute-start.15 = (bf16[480,768]{1,0:T(8,128)(2,1)S(1)}, bf16[480,768]{1,0:T(8,128)(2,1)S(1)}, u32[]{:S(2)}, u32[]{:S(2)}) collective-permute-start(bf16[480,768]{1,0:T(8,128)(2,1)S(1)} %bitcast.97), channel_id=1, source_target_pairs={{0,4},{4,0},{8,12},{12,8},{16,20},{20,16},{24,28},{28,24},{1,5},{5... | collective-permute-start | bytes 2211848 | tf_op jit(solution)/shard_map/ppermute | solution.py:28
  76.0 20.0 %collective-permute-start.18 = (bf16[480,768]{1,0:T(8,128)(2,1)S(1)}, bf16[480,768]{1,0:T(8,128)(2,1)}, u32[]{:S(2)}, u32[]{:S(2)}) collective-permute-start(bf16[480,768]{1,0:T(8,128)(2,1)S(1)} %collective-permute-done.13.refs_1_), channel_id=1, source_target_pairs={{0,16},{4,12},{8,24},{12,4},{16,0},{20,28},{24,8},{28,20},{1,17},{... | collective-permute-start | bytes 2211848 | tf_op jit(solution)/shard_map/ppermute | solution.py:28
  77.1 18.9 %collective-permute-start.16 = (bf16[480,768]{1,0:T(8,128)(2,1)S(1)}, bf16[480,768]{1,0:T(8,128)(2,1)}, u32[]{:S(2)}, u32[]{:S(2)}) collective-permute-start(bf16[480,768]{1,0:T(8,128)(2,1)S(1)} %collective-permute-done.13.refs_1_), channel_id=1, source_target_pairs={{0,4},{4,0},{8,12},{12,8},{16,20},{20,16},{24,28},{28,24},{1,5},{5... | collective-permute-start | bytes 2211848 | tf_op jit(solution)/shard_map/ppermute | solution.py:28
  77.1 18.9 %collective-permute-start.17 = (bf16[480,768]{1,0:T(8,128)(2,1)S(1)}, bf16[480,768]{1,0:T(8,128)(2,1)}, u32[]{:S(2)}, u32[]{:S(2)}) collective-permute-start(bf16[480,768]{1,0:T(8,128)(2,1)S(1)} %collective-permute-done.14.refs_2_), channel_id=1, source_target_pairs={{0,4},{4,0},{8,12},{12,8},{16,20},{20,16},{24,28},{28,24},{1,5},{5... | collective-permute-start | bytes 2211848 | tf_op jit(solution)/shard_map/ppermute | solution.py:28
  78.2 17.9 %copy-start.27 = (bf16[768]{0:T(1024)(128)(2,1)S(1)}, bf16[768]{0:T(1024)(128)(2,1)}, u32[]{:S(2)}) copy-start(bf16[768]{0:T(1024)(128)(2,1)} %param.27) | copy-start | bytes 4612
  78.2 17.9 %copy-start.28 = (bf16[768]{0:T(1024)(128)(2,1)S(1)}, bf16[768]{0:T(1024)(128)(2,1)}, u32[]{:S(2)}) copy-start(bf16[768]{0:T(1024)(128)(2,1)} %param.28) | copy-start | bytes 4612
  78.2 17.9 %copy-start.29 = (bf16[768]{0:T(1024)(128)(2,1)S(1)}, bf16[768]{0:T(1024)(128)(2,1)}, u32[]{:S(2)}) copy-start(bf16[768]{0:T(1024)(128)(2,1)} %param.33) | copy-start | bytes 4612
  78.2 18.0 %copy-start.30 = (bf16[768]{0:T(1024)(128)(2,1)S(1)}, bf16[768]{0:T(1024)(128)(2,1)}, u32[]{:S(2)}) copy-start(bf16[768]{0:T(1024)(128)(2,1)} %param.26) | copy-start | bytes 4612
  78.2 18.0 %copy-start.31 = (bf16[768]{0:T(1024)(128)(2,1)S(1)}, bf16[768]{0:T(1024)(128)(2,1)}, u32[]{:S(2)}) copy-start(bf16[768]{0:T(1024)(128)(2,1)} %param.32) | copy-start | bytes 4612
  78.2 18.0 %copy-start.32 = (bf16[768]{0:T(1024)(128)(2,1)S(1)}, bf16[768]{0:T(1024)(128)(2,1)}, u32[]{:S(2)}) copy-start(bf16[768]{0:T(1024)(128)(2,1)} %param.34) | copy-start | bytes 4612
  78.2 18.0 %copy-start.26 = (bf16[3072]{0:T(1024)(128)(2,1)S(1)}, bf16[3072]{0:T(1024)(128)(2,1)}, u32[]{:S(2)}) copy-start(bf16[3072]{0:T(1024)(128)(2,1)} %param.30) | copy-start | bytes 18436
  95.9 11.1 %collective-permute-start.19 = (bf16[480,768]{1,0:T(8,128)(2,1)}, bf16[480,768]{1,0:T(8,128)(2,1)}, u32[]{:S(2)}, u32[]{:S(2)}) collective-permute-start(bf16[480,768]{1,0:T(8,128)(2,1)} %collective-permute-done.18.refs_3_), channel_id=1, source_target_pairs={{0,4},{4,0},{8,12},{12,8},{16,20},{20,16},{24,28},{28,24},{1,5},{5... | collective-permute-start | bytes 2211848 | tf_op jit(solution)/shard_map/ppermute | solution.py:28
  153.8 12.8 %collective-permute-start.20 = (bf16[4,384,768]{2,1,0:T(8,128)(2,1)}, bf16[4,384,768]{2,1,0:T(8,128)(2,1)}, u32[]{:S(2)}, u32[]{:S(2)}) collective-permute-start(bf16[4,384,768]{2,1,0:T(8,128)(2,1)} %columns_term.2), channel_id=1, source_target_pairs={{0,4},{4,0},{8,12},{12,8},{16,20},{20,16},{24,28},{28,24},{1,5},{5... | collective-permute-start | bytes 7077896 | tf_op jit(solution)/shard_map/ppermute | solution.py:28
  166.6 19.9 %slice-start = ((s8[4718592]{0:T(1024)(128)(4,1)}), s8[4194304]{0:T(1024)(128)(4,1)S(1)}, s32[]{:S(2)}) async-start(s8[4718592]{0:T(1024)(128)(4,1)} %bitcast.116), calls=%async_computation.1 | async-start | bytes 8388608
  168.3 16.3 %collective-permute-start.21 = (bf16[2,384,768]{2,1,0:T(8,128)(2,1)S(1)}, bf16[2,384,768]{2,1,0:T(8,128)(2,1)S(1)}, u32[]{:S(2)}, u32[]{:S(2)}) collective-permute-start(bf16[2,384,768]{2,1,0:T(8,128)(2,1)S(1)} %add_convert_fusion.4), channel_id=1, source_target_pairs={{0,16},{4,12},{8,24},{12,4},{16,0},{20,28},{24,8},{28,20},{1,17},{... | collective-permute-start | bytes 3538952 | tf_op jit(solution)/shard_map/ppermute | solution.py:28
  168.4 18.1 %copy-start.7 = (f32[1024,768]{1,0:T(8,128)S(1)}, f32[1024,768]{1,0:T(8,128)}, u32[]{:S(2)}) copy-start(f32[1024,768]{1,0:T(8,128)} %copy-done.6) | copy-start | bytes 9437188
  168.4 18.1 %copy-start.9 = (f32[1024,768]{1,0:T(8,128)S(1)}, f32[1024,768]{1,0:T(8,128)}, u32[]{:S(2)}) copy-start(f32[1024,768]{1,0:T(8,128)} %copy-done.8) | copy-start | bytes 9437188
  168.4 18.1 %slice-start.1 = ((s8[4718592]{0:T(1024)(128)(4,1)}), s8[524288]{0:T(1024)(128)(4,1)S(1)}, s32[]{:S(2)}) async-start(s8[4718592]{0:T(1024)(128)(4,1)} %bitcast.116), calls=%async_computation.2 | async-start | bytes 1048576
  185.9 11.5 %collective-permute-start.22 = (bf16[384,768]{1,0:T(8,128)(2,1)S(1)}, bf16[384,768]{1,0:T(8,128)(2,1)S(1)}, u32[]{:S(2)}, u32[]{:S(2)}) collective-permute-start(bf16[384,768]{1,0:T(8,128)(2,1)S(1)} %fusion.7), channel_id=1, source_target_pairs={{0,8},{4,20},{8,0},{12,28},{16,24},{20,4},{24,16},{28,12},{1,9},{5... | collective-permute-start | bytes 1769480 | tf_op jit(solution)/shard_map/ppermute | solution.py:28
  213.7 19.8 %collective-permute-start.26 = (bf16[4,96,3840]{2,1,0:T(8,128)(2,1)}, bf16[4,96,3840]{2,1,0:T(8,128)(2,1)}, u32[]{:S(2)}, u32[]{:S(2)}) collective-permute-start(bf16[4,96,3840]{2,1,0:T(8,128)(2,1)} %get-tuple-element.114), channel_id=1, source_target_pairs={{0,4},{4,0},{8,12},{12,8},{16,20},{20,16},{24,28},{28,24},{1,5},{5... | collective-permute-start | bytes 8847368 | tf_op jit(solution)/shard_map/ppermute | solution.py:28
  213.7 14.1 %collective-permute-start.24 = (bf16[96,768]{1,0:T(8,128)(2,1)}, bf16[96,768]{1,0:T(8,128)(2,1)S(1)}, u32[]{:S(2)}, u32[]{:S(2)}) collective-permute-start(bf16[96,768]{1,0:T(8,128)(2,1)} %get-tuple-element.194), channel_id=1, source_target_pairs={{0,2},{1,3},{2,0},{3,1},{4,6},{5,7},{6,4},{7,5},{8,10},{9,11},{10,... | collective-permute-start | bytes 442376 | tf_op jit(solution)/shard_map/ppermute | solution.py:32
  213.7 14.1 %collective-permute-start.23 = (bf16[96,768]{1,0:T(8,128)(2,1)S(1)}, bf16[96,768]{1,0:T(8,128)(2,1)S(1)}, u32[]{:S(2)}, u32[]{:S(2)}) collective-permute-start(bf16[96,768]{1,0:T(8,128)(2,1)S(1)} %get-tuple-element.195), channel_id=1, source_target_pairs={{0,1},{1,2},{2,3},{3,0},{4,5},{5,6},{6,7},{7,4},{8,9},{9,10},{10,1... | collective-permute-start | bytes 442376 | tf_op jit(solution)/shard_map/ppermute | solution.py:32
  214.9 12.8 %collective-permute-start.25 = (bf16[96,768]{1,0:T(8,128)(2,1)S(1)}, bf16[96,768]{1,0:T(8,128)(2,1)S(1)}, u32[]{:S(2)}, u32[]{:S(2)}) collective-permute-start(bf16[96,768]{1,0:T(8,128)(2,1)S(1)} %get-tuple-element.193), channel_id=1, source_target_pairs={{0,3},{1,0},{2,1},{3,2},{4,7},{5,4},{6,5},{7,6},{8,11},{9,8},{10,9... | collective-permute-start | bytes 442376 | tf_op jit(solution)/shard_map/ppermute | solution.py:32
  236.3 20.0 %collective-permute-start.27 = (bf16[2,96,3840]{2,1,0:T(8,128)(2,1)}, bf16[2,96,3840]{2,1,0:T(8,128)(2,1)}, u32[]{:S(2)}, u32[]{:S(2)}) collective-permute-start(bf16[2,96,3840]{2,1,0:T(8,128)(2,1)} %add_convert_fusion.3), channel_id=1, source_target_pairs={{0,16},{4,12},{8,24},{12,4},{16,0},{20,28},{24,8},{28,20},{1,17},{... | collective-permute-start | bytes 4423688 | tf_op jit(solution)/shard_map/ppermute | solution.py:28
  237.1 19.2 %copy-start.15 = (bf16[4,96,3840]{2,1,0:T(8,128)(2,1)S(1)}, bf16[4,96,3840]{2,1,0:T(8,128)(2,1)}, u32[]{:S(2)}) copy-start(bf16[4,96,3840]{2,1,0:T(8,128)(2,1)} %get-tuple-element.109) | copy-start | bytes 8847364
  258.8 19.5 %collective-permute-start.28 = (bf16[96,3840]{1,0:T(8,128)(2,1)}, bf16[96,3840]{1,0:T(8,128)(2,1)}, u32[]{:S(2)}, u32[]{:S(2)}) collective-permute-start(bf16[96,3840]{1,0:T(8,128)(2,1)} %fusion.6), channel_id=1, source_target_pairs={{0,8},{4,20},{8,0},{12,28},{16,24},{20,4},{24,16},{28,12},{1,9},{5... | collective-permute-start | bytes 2211848 | tf_op jit(solution)/shard_map/ppermute | solution.py:28
  281.4 16.6 %copy-start.12 = (bf16[1024,768]{1,0:T(8,128)(2,1)S(1)}, bf16[1024,768]{1,0:T(8,128)(2,1)}, u32[]{:S(2)}) copy-start(bf16[1024,768]{1,0:T(8,128)(2,1)} %get-tuple-element.123) | copy-start | bytes 4718596
  289.3 14.1 %copy-start.17 = (bf16[24,3840]{1,0:T(8,128)(2,1)S(1)}, bf16[24,3840]{1,0:T(8,128)(2,1)}, u32[]{:S(2)}) copy-start(bf16[24,3840]{1,0:T(8,128)(2,1)} %get-tuple-element.185) | copy-start | bytes 552964
  289.3 11.3 %collective-permute-start.29 = (bf16[4,96,2304]{2,1,0:T(8,128)(2,1)}, bf16[4,96,2304]{2,1,0:T(8,128)(2,1)}, u32[]{:S(2)}, u32[]{:S(2)}) collective-permute-start(bf16[4,96,2304]{2,1,0:T(8,128)(2,1)} %get-tuple-element.129), channel_id=1, source_target_pairs={{0,4},{4,0},{8,12},{12,8},{16,20},{20,16},{24,28},{28,24},{1,5},{5... | collective-permute-start | bytes 5308424 | tf_op jit(solution)/shard_map/ppermute | solution.py:28
  292.9 19.3 %copy-start.21 = (f32[1024]{0:T(1024)S(1)}, f32[1024]{0:T(1024)}, u32[]{:S(2)}) copy-start(f32[1024]{0:T(1024)} %copy-done.20) | copy-start | bytes 12292
  302.0 1.3 collective-permute-start.31
  303.3 7.9 %collective-permute-start.33 = (f32[12,768]{1,0:T(8,128)S(1)}, f32[12,768]{1,0:T(8,128)S(1)}, u32[]{:S(2)}, u32[]{:S(2)}) collective-permute-start(f32[12,768]{1,0:T(8,128)S(1)} %add.305), channel_id=1, source_target_pairs={{0,16},{4,12},{8,24},{12,4},{16,0},{20,28},{24,8},{28,20},{1,17},{... | collective-permute-start | bytes 110600 | tf_op jit(solution)/shard_map/ppermute | solution.py:28
  303.4 23.2 %collective-permute-start.43 = (bf16[24,3840]{1,0:T(8,128)(2,1)S(1)}, bf16[24,3840]{1,0:T(8,128)(2,1)S(1)}, u32[]{:S(2)}, u32[]{:S(2)}) collective-permute-start(bf16[24,3840]{1,0:T(8,128)(2,1)S(1)} %copy-done.17), channel_id=1, source_target_pairs={{0,3},{1,0},{2,1},{3,2},{4,7},{5,4},{6,5},{7,6},{8,11},{9,8},{10,9... | collective-permute-start | bytes 552968 | tf_op jit(solution)/shard_map/ppermute | solution.py:32
  303.5 23.1 %collective-permute-start.42 = (bf16[24,3840]{1,0:T(8,128)(2,1)}, bf16[24,3840]{1,0:T(8,128)(2,1)S(1)}, u32[]{:S(2)}, u32[]{:S(2)}) collective-permute-start(bf16[24,3840]{1,0:T(8,128)(2,1)} %get-tuple-element.183), channel_id=1, source_target_pairs={{0,2},{1,3},{2,0},{3,1},{4,6},{5,7},{6,4},{7,5},{8,10},{9,11},{10,... | collective-permute-start | bytes 552968 | tf_op jit(solution)/shard_map/ppermute | solution.py:32
  309.9 16.7 %collective-permute-start.41 = (bf16[24,3840]{1,0:T(8,128)(2,1)}, bf16[24,3840]{1,0:T(8,128)(2,1)S(1)}, u32[]{:S(2)}, u32[]{:S(2)}) collective-permute-start(bf16[24,3840]{1,0:T(8,128)(2,1)} %get-tuple-element.184), channel_id=1, source_target_pairs={{0,1},{1,2},{2,3},{3,0},{4,5},{5,6},{6,7},{7,4},{8,9},{9,10},{10,1... | collective-permute-start | bytes 552968 | tf_op jit(solution)/shard_map/ppermute | solution.py:32
  309.9 18.8 %collective-permute-start.30 = (bf16[2,96,2304]{2,1,0:T(8,128)(2,1)S(1)}, bf16[2,96,2304]{2,1,0:T(8,128)(2,1)S(1)}, u32[]{:S(2)}, u32[]{:S(2)}) collective-permute-start(bf16[2,96,2304]{2,1,0:T(8,128)(2,1)S(1)} %add_convert_fusion.5), channel_id=1, source_target_pairs={{0,16},{4,12},{8,24},{12,4},{16,0},{20,28},{24,8},{28,20},{1,17},{... | collective-permute-start | bytes 2654216 | tf_op jit(solution)/shard_map/ppermute | solution.py:28
  311.3 15.3 %collective-permute-start.37 = (f32[12,768]{1,0:T(8,128)S(1)}, f32[12,768]{1,0:T(8,128)S(1)}, u32[]{:S(2)}, u32[]{:S(2)}) collective-permute-start(f32[12,768]{1,0:T(8,128)S(1)} %add.310), channel_id=1, source_target_pairs={{0,8},{4,20},{8,0},{12,28},{16,24},{20,4},{24,16},{28,12},{1,9},{5... | collective-permute-start | bytes 110600 | tf_op jit(solution)/shard_map/ppermute | solution.py:28
  326.6 6.9 %collective-permute-start.40 = (f32[12,768]{1,0:T(8,128)S(1)}, f32[12,768]{1,0:T(8,128)S(1)}, u32[]{:S(2)}, u32[]{:S(2)}) collective-permute-start(f32[12,768]{1,0:T(8,128)S(1)} %add.312), channel_id=1, source_target_pairs={{0,3},{1,0},{2,1},{3,2},{4,7},{5,4},{6,5},{7,6},{8,11},{9,8},{10,9... | collective-permute-start | bytes 110600 | tf_op jit(solution)/shard_map/ppermute | solution.py:32
  326.7 6.8 %collective-permute-start.39 = (f32[12,768]{1,0:T(8,128)S(1)}, f32[12,768]{1,0:T(8,128)S(1)}, u32[]{:S(2)}, u32[]{:S(2)}) collective-permute-start(f32[12,768]{1,0:T(8,128)S(1)} %add.312), channel_id=1, source_target_pairs={{0,2},{1,3},{2,0},{3,1},{4,6},{5,7},{6,4},{7,5},{8,10},{9,11},{10,... | collective-permute-start | bytes 110600 | tf_op jit(solution)/shard_map/ppermute | solution.py:32
  326.8 6.9 %collective-permute-start.38 = (f32[12,768]{1,0:T(8,128)S(1)}, f32[12,768]{1,0:T(8,128)S(1)}, u32[]{:S(2)}, u32[]{:S(2)}) collective-permute-start(f32[12,768]{1,0:T(8,128)S(1)} %add.312), channel_id=1, source_target_pairs={{0,1},{1,2},{2,3},{3,0},{4,5},{5,6},{6,7},{7,4},{8,9},{9,10},{10,1... | collective-permute-start | bytes 110600 | tf_op jit(solution)/shard_map/ppermute | solution.py:32
  329.9 8.4 %collective-permute-start.32 = (bf16[96,2304]{1,0:T(8,128)(2,1)S(1)}, bf16[96,2304]{1,0:T(8,128)(2,1)S(1)}, u32[]{:S(2)}, u32[]{:S(2)}) collective-permute-start(bf16[96,2304]{1,0:T(8,128)(2,1)S(1)} %fusion.8), channel_id=1, source_target_pairs={{0,8},{4,20},{8,0},{12,28},{16,24},{20,4},{24,16},{28,12},{1,9},{5... | collective-permute-start | bytes 1327112 | tf_op jit(solution)/shard_map/ppermute | solution.py:28
  340.9 6.8 %collective-permute-start.36 = (bf16[96,576]{0,1:T(8,128)(2,1)S(1)}, bf16[96,576]{0,1:T(8,128)(2,1)S(1)}, u32[]{:S(2)}, u32[]{:S(2)}) collective-permute-start(bf16[96,576]{0,1:T(8,128)(2,1)S(1)} %get-tuple-element.190), channel_id=1, source_target_pairs={{0,3},{1,0},{2,1},{3,2},{4,7},{5,4},{6,5},{7,6},{8,11},{9,8},{10,9... | collective-permute-start | bytes 331784 | tf_op jit(solution)/shard_map/ppermute | solution.py:32
  343.3 12.4 %collective-permute-start.35 = (bf16[96,576]{0,1:T(8,128)(2,1)S(1)}, bf16[96,576]{0,1:T(8,128)(2,1)S(1)}, u32[]{:S(2)}, u32[]{:S(2)}) collective-permute-start(bf16[96,576]{0,1:T(8,128)(2,1)S(1)} %get-tuple-element.191), channel_id=1, source_target_pairs={{0,2},{1,3},{2,0},{3,1},{4,6},{5,7},{6,4},{7,5},{8,10},{9,11},{10,... | collective-permute-start | bytes 331784 | tf_op jit(solution)/shard_map/ppermute | solution.py:32
  344.0 11.8 %collective-permute-start.34 = (bf16[96,576]{0,1:T(8,128)(2,1)S(1)}, bf16[96,576]{0,1:T(8,128)(2,1)S(1)}, u32[]{:S(2)}, u32[]{:S(2)}) collective-permute-start(bf16[96,576]{0,1:T(8,128)(2,1)S(1)} %get-tuple-element.192), channel_id=1, source_target_pairs={{0,1},{1,2},{2,3},{3,0},{4,5},{5,6},{6,7},{7,4},{8,9},{9,10},{10,1... | collective-permute-start | bytes 331784 | tf_op jit(solution)/shard_map/ppermute | solution.py:32
  (20 other events, 82.3 us)
Sparse Core Ops, SparseCore 0:
  18.7 80.7 all-gather.1
where the time goes:
time: 369 us; the launch traced here: 365 us
  Pallas kernels  110 us (30%)
  waiting for transfers between devices  59.8 us (16%)
  matrix products  59.6 us (16%)
  starting transfers between devices  55.6 us (15%)
  other arithmetic  36.1 us (10%)
  local copies, waits for them, and re-layouts  29 us (8%)
  between operations  15.1 us (4%)
    pallas_call x4, Pallas kernels, attend(): pl.pallas_call(functools.partial(kernel, block), grid_spec=pltpu.Prefetch...  61.7 us
    ppermute x18, waiting for transfers between devices, shift_line(): return lax.ppermute(value, 'heads', [(i, (i + step) % 4) for i in range(4)])  38.7 us
    dot_general x4, matrix products, dot_lanes(): lax.dot_general(left, right, (((1,), (1,)), ((), ())), preferred_element_...  37.8 us
    ppermute x18, starting transfers between devices, shift_line(): return lax.ppermute(value, 'heads', [(i, (i + step) % 4) for i in range(4)])  29.4 us
    ppermute x26, starting transfers between devices, exchange(): return lax.ppermute(value, 'rows', [(i, i ^ bits[i & 1]) for i in range(8)])  26.1 us
    dot_general x3, matrix products, dot_plain(): lax.dot_general(left, right, (((1,), (0,)), ((), ())), preferred_element_...  21.9 us
    ppermute x26, waiting for transfers between devices, exchange(): return lax.ppermute(value, 'rows', [(i, i ^ bits[i & 1]) for i in range(8)])  21 us
    pallas_call x2, Pallas kernels, rows_terms(): pl.pallas_call(kernel, grid_spec=pltpu.PrefetchScalarGridSpec(num_scalar_...  20 us
  transfers between devices with their start and end apart: 45, of which 17 were waited for; matrix products, arithmetic and copies ran while one was open for 21% of the time, Pallas kernels for 23%

commit v1 on v0

--- a/solution.py
+++ b/solution.py
@@ -179,35 +179,6 @@
     )(order, tokens, bias, *pieces)
 
 
-def join_kernel(order, *refs):
-    pieces, (output_full, inner_full, semaphores) = refs[:8], refs[8:]
-    depth, width = output_full.shape[1:]
-    moves = []
-    for slot in range(8):
-        moves.append((pieces[slot].at[pl.ds(0, depth)], output_full.at[order[slot]]))
-        for column in range(inner_full.shape[2] // width):
-            source = pieces[slot].at[pl.ds(depth * (1 + column), depth)]
-            target = inner_full.at[order[slot], :, pl.ds(column * width, width)]
-            moves.append((source, target))
-    copy_all(moves, semaphores)
-
-
-def join(order, pieces, depth, columns):
-    width = pieces[0].shape[1]
-    shapes = [(8, depth, width), (8, depth, columns * width)]
-    size = pieces[0].size * 8
-    return pl.pallas_call(
-        join_kernel,
-        in_specs=[pl.BlockSpec(memory_space=pltpu.SMEM)] + [HBM] * 8,
-        out_specs=[pl.BlockSpec(memory_space=pltpu.VMEM)] * 2,
-        out_shape=tuple(jax.ShapeDtypeStruct(shape, BF16) for shape in shapes),
-        scratch_shapes=[pltpu.SemaphoreType.DMA((8 * (columns + 1),))],
-        compiler_params=WIDE,
-        cost_estimate=pl.CostEstimate(flops=0, bytes_accessed=4 * size, transcendentals=0),
-        name="join",
-    )(order, *pieces)
-
-
 def rows_terms_kernel(parts, order, *refs):
     lefts, rights = refs[:parts], refs[parts : 2 * parts]
     send_ref, keep_ref, turned, product = refs[2 * parts :]
@@ -347,8 +318,8 @@
         got = self.dense_got
         (last,) = behind(core_gather(got[3:]), (context,))
         pieces = self.dense_mine + got[3:] + got[:3] + (last,)
-        fulls = join(self.order, pieces, self.dense_depth, self.columns)
-        return tuple(full.reshape(-1, full.shape[2]) for full in fulls) + (self.outer_full,)
+        outer = self.outer_full.reshape(self.columns, -1, self.outer_full.shape[1])
+        return load_slots, 8 * (self.columns + 1) + 1, self.order, pieces + (outer,)
 
     def outer_terms(self, hidden_low, branch_grad):
         send = columns_term(hidden_low, branch_grad, self.away)
@@ -356,15 +327,20 @@
         return keep, self.begin(scatter_steps(send, keep, stack_rows))
 
     def inner_terms(self, inner_pair, output_pair):
-        terms = rows_terms((inner_pair, output_pair), self.order)
-        return terms[1], self.begin(scatter_steps(*terms, stack_rows))
+        return rows_terms((inner_pair, output_pair), self.order)
+
+    def inner_steps(self, terms, gate):
+        send, keep = terms
+        return self.begin(scatter_steps(after(send, gate), keep, stack_rows))
 
     def inner_cut(self, both):
         cut = self.columns * both.shape[1] // (self.columns + 1)
         return both[:, :cut], both[:, cut:]
 
     def packed_terms(self, tokens, packed_grad):
-        terms = rows_terms(((tokens, packed_grad),), self.order)
+        return rows_terms(((tokens, packed_grad),), self.order)
+
+    def packed_steps(self, terms):
         return self.begin(scatter_steps(*terms, stack_columns))
 
     def begin(self, steps):
@@ -418,7 +394,15 @@
         return packed
 
     def dense(self, context):
-        return self.fulls
+        output, inner, outer = self.fulls
+        width = output.shape[1]
+        chunks = inner.shape[1] // width
+        sources = (
+            output.reshape(8, -1, width),
+            inner.reshape(8, -1, inner.shape[1]),
+            outer.reshape(chunks, -1, width),
+        )
+        return load_whole, 2 + chunks, jnp.zeros((8,), jnp.int32), sources
 
     def scatter(self, term):
         return lax.psum_scatter(term, ("rows", "heads"), scatter_dimension=0, tiled=True)
@@ -427,8 +411,10 @@
         return None, self.scatter(dot_rows(hidden_low, branch_grad))
 
     def inner_terms(self, inner_pair, output_pair):
-        both = self.scatter(dot_rows(*inner_pair)), self.scatter(dot_rows(*output_pair))
-        return None, both
+        return self.scatter(dot_rows(*inner_pair)), self.scatter(dot_rows(*output_pair))
+
+    def inner_steps(self, terms, gate):
+        return terms
 
     def inner_cut(self, both):
         return both
@@ -441,6 +427,9 @@
         return tuple(
             lax.psum_scatter(p, "rows", scatter_dimension=0, tiled=True) for p in parts
         )
+
+    def packed_steps(self, terms):
+        return terms
 
     def packed_cut(self, total):
         return total
@@ -610,15 +599,155 @@
     return attend(backward_kernel, block, kinds, operands, earlier, outs, cost, "attend_backward")
 
 
-def gelu_exact(inner):
-    return 0.5 * inner * (1.0 + lax.erf(inner * 0.7071067811865476))
-
-
-def norm_apply(hidden_in, norm_gain, norm_shift):
-    average = jnp.mean(hidden_in, axis=-1, keepdims=True)
-    centred = hidden_in - average
-    variance = jnp.mean(centred * centred, axis=-1, keepdims=True)
-    return centred * lax.rsqrt(variance + EPSILON) * norm_gain + norm_shift
+def norm_parts(value):
+    average = jnp.mean(value, axis=-1, keepdims=True)
+    centred = value - average
+    scale = lax.rsqrt(jnp.mean(centred * centred, axis=-1, keepdims=True) + EPSILON)
+    return centred * scale, scale
+
+
+def norm_back(grad, gain, normed, scale):
+    inner = grad * gain
+    average = jnp.mean(inner, axis=-1, keepdims=True)
+    along = jnp.mean(inner * normed, axis=-1, keepdims=True)
+    return scale * (inner - average - normed * along)
+
+
+def row_sum(value):
+    return jnp.sum(value, axis=0, keepdims=True)
+
+
+def dense_kernel(load, kinds, order, context, tokens, cotangent, vectors, *refs):
+    count = len(refs) - 14
+    sources = refs[:count]
+    layer_out, hidden, branch, first_low, inner_grad, attended, first_grad, context_grad, sums = (
+        refs[count : count + 9]
+    )
+    output_full, inner_full, outer_full, slopes, semaphores = refs[count + 9 :]
+    step = pl.program_id(0)
+    chunks, width = inner_full.shape[0], context.shape[1]
+
+    @pl.when(step == 0)
+    def _():
+        copy_all(load(order, sources, output_full, inner_full, outer_full), semaphores)
+        sums[...] = jnp.zeros_like(sums)
+
+    def vector(row):
+        return vectors[pl.ds(row, 1), :]
+
+    def add(row, value):
+        sums[pl.ds(row, 1), :] += row_sum(value)
+
+    output_weight = output_full[...].reshape(width, width)
+    attended_out = dot_plain(context[...], output_weight) + vector(0)
+    first_normed, first_scale = norm_parts(tokens[...].astype(F32) + attended_out)
+    first_out = first_normed * vector(1) + vector(2)
+    low = first_out.astype(BF16)
+    first_low[...] = low
+    second = first_out + vector(3)
+    for chunk in range(chunks):
+        columns = pl.ds(chunk * width, width)
+        inner = dot_plain(low, inner_full[chunk].reshape(width, width)) + vector(6 + chunk)
+        half = 0.5 * (1.0 + lax.erf(inner * 0.7071067811865476))
+        slopes[:, columns] = half + inner * jnp.exp(-0.5 * inner * inner) * 0.3989422804014327
+        hidden_low = (inner * half).astype(BF16)
+        hidden[:, columns] = hidden_low
+        second = second + dot_plain(hidden_low, outer_full[chunk])
+    normed, scale = norm_parts(second)
+    block = step * context.shape[0] // BLOCK
+    valid = jnp.where(kinds[block] != 2, 1.0, 0.0).astype(F32)
+    layer_out[...] = ((normed * vector(4) + vector(5)) * valid).astype(BF16)
+    out_grad = cotangent[...].astype(F32) * valid
+    add(4, out_grad * normed)
+    add(5, out_grad)
+    second_grad = norm_back(out_grad, vector(4), normed, scale)
+    branch_low = second_grad.astype(BF16)
+    branch[...] = branch_low
+    add(3, branch_low.astype(F32))
+    first_out_grad = second_grad
+    for chunk in range(chunks):
+        columns = pl.ds(chunk * width, width)
+        hidden_grad = dot_lanes(branch_low, outer_full[chunk])
+        inner_low = (hidden_grad * slopes[:, columns]).astype(BF16)
+        inner_grad[:, columns] = inner_low
+        add(6 + chunk, inner_low.astype(F32))
+        first_out_grad = first_out_grad + dot_lanes(
+            inner_low, inner_full[chunk].reshape(width, width)
+        )
+    add(1, first_out_grad * first_normed)
+    add(2, first_out_grad)
+    grad = norm_back(first_out_grad, vector(1), first_normed, first_scale)
+    first_grad[...] = grad
+    attended_low = grad.astype(BF16)
+    attended[...] = attended_low
+    add(0, attended_low.astype(F32))
+    context_grad[...] = dot_lanes(attended_low, output_weight).astype(BF16)
+
+
+def dense(load, copies, kinds, order, context, tokens, cotangent, vectors, sources):
+    count, width = tokens.shape
+    chunks = vectors.shape[0] - 6
+    tile = 256
+    narrow = pl.BlockSpec((tile, width), lambda i, *_: (i, 0))
+    wide = pl.BlockSpec((tile, chunks * width), lambda i, *_: (i, 0))
+    fixed = pl.BlockSpec(vectors.shape, lambda i, *_: (0, 0))
+    low = jax.ShapeDtypeStruct((count, width), BF16)
+    low_wide = jax.ShapeDtypeStruct((count, chunks * width), BF16)
+    return pl.pallas_call(
+        functools.partial(dense_kernel, load),
+        grid_spec=pltpu.PrefetchScalarGridSpec(
+            num_scalar_prefetch=2,
+            grid=(count // tile,),
+            in_specs=[narrow, narrow, narrow, fixed] + [HBM] * len(sources),
+            out_specs=[narrow, wide, narrow, narrow, wide, narrow, narrow, narrow, fixed],
+            scratch_shapes=[
+                pltpu.VMEM((8, width // 8, width), BF16),
+                pltpu.VMEM((chunks, 8, width // 8, width), BF16),
+                pltpu.VMEM((chunks, width, width), BF16),
+                pltpu.VMEM((tile, chunks * width), F32),
+                pltpu.SemaphoreType.DMA((copies,)),
+            ],
+        ),
+        out_shape=(
+            low,
+            low_wide,
+            low,
+            low,
+            low_wide,
+            low,
+            jax.ShapeDtypeStruct((count, width), F32),
+            low,
+            jax.ShapeDtypeStruct(vectors.shape, F32),
+        ),
+        compiler_params=WIDE,
+        cost_estimate=pl.CostEstimate(
+            flops=4 * count * width * width * (1 + 2 * chunks),
+            bytes_accessed=2 * count * width * (10 + 2 * chunks),
+            transcendentals=2 * count * width * chunks,
+        ),
+        name="dense",
+    )(kinds, order, context, tokens, cotangent, vectors, *sources)
+
+
+def load_slots(order, sources, output_full, inner_full, outer_full):
+    pieces, outer = sources[:8], sources[8]
+    depth = output_full.shape[1]
+    moves = []
+    for slot in range(8):
+        moves.append((pieces[slot].at[pl.ds(0, depth)], output_full.at[order[slot]]))
+        for chunk in range(inner_full.shape[0]):
+            source = pieces[slot].at[pl.ds(depth * (1 + chunk), depth)]
+            moves.append((source, inner_full.at[chunk, order[slot]]))
+    return moves + [(outer, outer_full)]
+
+
+def load_whole(order, sources, output_full, inner_full, outer_full):
+    output, inner, outer = sources
+    width = output.shape[2]
+    moves = [(output, output_full), (outer, outer_full)]
+    for chunk in range(inner_full.shape[0]):
+        moves.append((inner.at[:, :, pl.ds(chunk * width, width)], inner_full.at[chunk]))
+    return moves
 
 
 def shards(
@@ -646,8 +775,8 @@
     kinds = lax.dynamic_slice_in_dim(
         block_kind, lax.axis_index("heads") * per_device, per_device
     )
-    valid = jnp.repeat((kinds != 2).astype(F32), BLOCK)[:, None]
-
+    singles = (output_bias, first_gain, first_shift, outer_bias, second_gain, second_shift)
+    vectors = jnp.concatenate([jnp.stack(singles), inner_bias.reshape(-1, width)]).astype(F32)
     eight_by_four = lax.axis_size("rows") == 8 and lax.axis_size("heads") == 4
     moves = SlotMoves() if eight_by_four else PlainMoves()
     moves.gather(
@@ -662,91 +791,66 @@
             packed = moves.dense_start(packed, earlier)
         earlier = attend_forward(block, kinds, packed, earlier)
     context, totals = earlier
-    output_full, inner_full, outer_full = moves.dense(context)
-
-    attended = dot_plain(context, output_full) + output_bias
-    first_sum = tokens.astype(F32) + attended
-    first_out = norm_apply(first_sum, first_gain, first_shift)
-    first_low = first_out.astype(BF16)
-    inner_pre = dot_plain(first_low, inner_full) + inner_bias
-    hidden_low = gelu_exact(inner_pre).astype(BF16)
-    second_sum = first_out + (dot_plain(hidden_low, outer_full) + outer_bias)
-    final = norm_apply(second_sum, second_gain, second_shift)
-    layer_out = (final * valid).astype(BF16)
-
-    out_grad = cotangent.astype(F32) * valid
-    _, second_pull = jax.vjp(
-        norm_apply, second_sum, second_gain.astype(F32), second_shift.astype(F32)
-    )
-    second_grad, second_gain_grad, second_shift_grad = second_pull(out_grad)
-    branch_grad = second_grad.astype(BF16)
+    load, copies, order, sources = moves.dense(context)
+    (
+        layer_out,
+        hidden_low,
+        branch_grad,
+        first_low,
+        inner_grad,
+        attended_grad,
+        first_grad,
+        context_grad,
+        sums,
+    ) = dense(load, copies, kinds, order, context, tokens, cotangent, vectors, sources)
+
     kernel_done, outer_steps = moves.outer_terms(hidden_low, branch_grad)
-    outer_bias_grad = jnp.sum(branch_grad, axis=0, dtype=F32)
-    branch_grad = moves.behind(branch_grad, outer_steps, kernel_done)
-    hidden_grad = dot_lanes(branch_grad, outer_full)
-    _, gelu_pull = jax.vjp(gelu_exact, inner_pre)
-    inner_grad = gelu_pull(hidden_grad)[0].astype(BF16)
-    inner_bias_grad = jnp.sum(inner_grad, axis=0, dtype=F32)
-    inner_grad = moves.behind(inner_grad, outer_steps, inner_grad)
-    first_out_grad = second_grad + dot_lanes(inner_grad, inner_full)
-    _, first_pull = jax.vjp(
-        norm_apply, first_sum, first_gain.astype(F32), first_shift.astype(F32)
-    )
-    first_grad, first_gain_grad, first_shift_grad = first_pull(first_out_grad)
-    attended_grad = first_grad.astype(BF16)
-    output_bias_grad = jnp.sum(attended_grad, axis=0, dtype=F32)
-    terms_grad = moves.behind(attended_grad, outer_steps, attended_grad)
-    kernel_done, inner_steps = moves.inner_terms((first_low, inner_grad), (context, terms_grad))
-    outer_weight_grad = moves.finish(outer_steps, kernel_done)
-    attended_grad = moves.hold(attended_grad, outer_weight_grad)
-    context_grad = dot_lanes(attended_grad, output_full).astype(BF16)
-    context_grad = moves.behind(context_grad, inner_steps, context_grad)
+    inner_grad = moves.behind(inner_grad, outer_steps, kernel_done)
+    inner_terms = moves.inner_terms((first_low, inner_grad), (context, attended_grad))
+    context_grad = moves.behind(context_grad, outer_steps, inner_terms[1])
+    inner_steps = moves.inner_steps(inner_terms, context_grad)
     pieces = None
     for block in range(per_device):
-        if block > 0:
+        if block == per_device - 1:
+            context_grad = moves.behind(context_grad, outer_steps, pieces[0])
             context_grad = moves.behind(context_grad, inner_steps, pieces[0])
         pieces = attend_backward(block, kinds, packed, context, context_grad, totals, pieces)
+    outer_weight_grad = moves.finish(outer_steps, pieces[0])
     packed_grad = jnp.concatenate(pieces, axis=1)
     packed_grad = moves.behind(packed_grad, inner_steps, pieces[0])
-    packed_steps = moves.packed_terms(tokens, packed_grad)
-    sums = (
-        jnp.sum(pieces[0], axis=0, dtype=F32),
-        jnp.sum(pieces[2], axis=0, dtype=F32),
-        output_bias_grad,
-        first_gain_grad,
-        first_shift_grad,
-        outer_bias_grad,
-        second_gain_grad,
-        second_shift_grad,
-    )
-    inner_rows = inner_bias_grad.reshape(-1, width)
+    packed_grad = moves.hold(packed_grad, outer_weight_grad)
+    packed_terms = moves.packed_terms(tokens, packed_grad)
+    packed_steps = moves.packed_steps(packed_terms)
+    inner_ready = moves.behind(packed_terms[1], inner_steps, packed_terms[1])
+    bias_sums = jnp.stack([jnp.sum(pieces[i], axis=0, dtype=F32) for i in (0, 2)])
 
     def tokens_part(gate):
-        return first_grad + dot_lanes(after(packed_grad, gate), packed_weight)
+        return first_grad + dot_lanes(after(packed_grad, gate, inner_ready), packed_weight)
 
     tokens_grad, packed_total, small, inner_both = moves.last(
-        tokens_part, packed_steps, jnp.concatenate([jnp.stack(sums), inner_rows]), inner_steps
+        tokens_part, packed_steps, jnp.concatenate([sums, bias_sums]), inner_steps
     )
     inner_weight_grad, output_weight_grad = moves.inner_cut(inner_both)
     query_weight_grad, key_weight_grad, value_weight_grad = moves.packed_cut(packed_total)
+    rows = sums.shape[0]
     return (
         layer_out,
         tokens_grad,
         query_weight_grad,
         key_weight_grad,
         value_weight_grad,
+        small[rows],
+        small[rows + 1],
+        output_weight_grad,
         small[0],
         small[1],
-        output_weight_grad,
         small[2],
+        inner_weight_grad,
+        small[6:rows].reshape(-1),
+        outer_weight_grad,
         small[3],
         small[4],
-        inner_weight_grad,
-        small[len(sums) :].reshape(-1),
-        outer_weight_grad,
         small[5],
-        small[6],
-        small[7],
     )
 
 

time: 369 us -> 323 us (0.88); the launches traced: 365 us -> 323 us
  matrix products: 59.6 us -> 6.66 us
  Pallas kernels: 110 us -> 133 us
  other arithmetic: 36.1 us -> 17.1 us
  waiting for transfers between devices: 59.8 us -> 70.7 us
  local copies, waits for them, and re-layouts: 29 us -> 18.4 us
  starting transfers between devices: 55.6 us -> 62.7 us
    pallas_call x1, Pallas kernels: 6.08 us -> 41.6 us  [dense(): pl.pallas_call(functools.partial(dense_kernel, load), grid_spec=pltpu.Pre...]
    dot_general x4 -> x1, matrix products: 37.8 us -> 6.66 us  [dot_lanes(): lax.dot_general(left, right, (((1,), (1,)), ((), ())), preferred_element_...]
    dot_general x3 -> x0, matrix products: 21.9 us -> none  [dot_plain(): lax.dot_general(left, right, (((1,), (0,)), ((), ())), preferred_element_...]
    ppermute x26, waiting for transfers between devices: 21 us -> 35.8 us  [exchange(): return lax.ppermute(value, 'rows', [(i, i ^ bits[i & 1]) for i in range(8)])]
    pallas_call x4, Pallas kernels: 61.7 us -> 50 us  [attend(): pl.pallas_call(functools.partial(kernel, block), grid_spec=pltpu.Prefetch...]
    reduce_sum x8 -> x1, other arithmetic: 10.6 us -> 0.49 us  [shards(): jnp.sum(pieces[i], axis=0, dtype=F32)]
    ppermute x26, starting transfers between devices: 26.1 us -> 31.2 us  [exchange(): return lax.ppermute(value, 'rows', [(i, i ^ bits[i & 1]) for i in range(8)])]
    reshape x6 -> x2, local copies, waits for them, and re-layouts: 4.46 us -> 0.62 us  [the longest x1 0.61 us: shards(): small[6:rows].reshape(-1)]
  transfers between devices with their start and end apart: 45 -> 45, of which waited for: 17 -> 18; matrix products, arithmetic and copies ran while one was open for 21% -> 8% of each run, Pallas kernels for 23% -> 24%
where the time goes in v1:
time: 323 us
  Pallas kernels  133 us (41%)
  waiting for transfers between devices  70.7 us (22%)
  starting transfers between devices  62.7 us (19%)
  local copies, waits for them, and re-layouts  18.4 us (6%)
  other arithmetic  17.1 us (5%)
  between operations  14.7 us (5%)
  matrix products  6.66 us (2%)
    pallas_call x4, Pallas kernels, attend(): pl.pallas_call(functools.partial(kernel, block), grid_spec=pltpu.Prefetch...  50 us
    pallas_call x1, Pallas kernels, dense(): pl.pallas_call(functools.partial(dense_kernel, load), grid_spec=pltpu.Pre...  41.6 us
    ppermute x26, waiting for transfers between devices, exchange(): return lax.ppermute(value, 'rows', [(i, i ^ bits[i & 1]) for i in range(8)])  35.8 us
    ppermute x18, waiting for transfers between devices, shift_line(): return lax.ppermute(value, 'heads', [(i, (i + step) % 4) for i in range(4)])  34.9 us
    ppermute x18, starting transfers between devices, shift_line(): return lax.ppermute(value, 'heads', [(i, (i + step) % 4) for i in range(4)])  31.4 us
    ppermute x26, starting transfers between devices, exchange(): return lax.ppermute(value, 'rows', [(i, i ^ bits[i & 1]) for i in range(8)])  31.2 us
    pallas_call x2, Pallas kernels, rows_terms(): pl.pallas_call(kernel, grid_spec=pltpu.PrefetchScalarGridSpec(num_scalar_...  19.6 us
    unnamed x70, local copies, waits for them, and re-layouts  12 us
  transfers between devices with their start and end apart: 45, of which 18 were waited for; matrix products, arithmetic and copies ran while one was open for 8% of the time, Pallas kernels for 24%

profile of v1, /device:TPU:0, one launch (start us, length us, event | category | flops | bytes accessed | tf_op | source)
XLA Modules:
  0.0 323.0 jit_solution(5860460405483101004)
XLA Ops:
  7.2 0.9 copy.49
  8.1 0.9 copy.50
  9.1 0.9 copy.51
  10.0 5.1 %collective-permute-start.3 = (bf16[96,576]{0,1:T(8,128)(2,1)S(1)}, bf16[96,576]{0,1:T(8,128)(2,1)S(1)}, u32[]{:S(2)}, u32[]{:S(2)}) collective-permute-start(bf16[96,576]{0,1:T(8,128)(2,1)S(1)} %pad_maximum_fusion.2), channel_id=1, source_target_pairs={{0,3},{1,0},{2,1},{3,2},{4,7},{5,4},{6,5},{7,6},{8,11},{9,8},{10,9... | collective-permute-start | bytes 331784 | tf_op jit(solution)/shard_map/ppermute | solution.py:32
  15.1 3.4 %collective-permute-done.3 = bf16[96,576]{0,1:T(8,128)(2,1)S(1)} collective-permute-done((bf16[96,576]{0,1:T(8,128)(2,1)S(1)}, bf16[96,576]{0,1:T(8,128)(2,1)S(1)}, u32[]{:S(2)}, u32[]{:S(2)}) %collective-permute-start.3) | collective-permute-done | bytes 110624 | tf_op jit(solution)/shard_map/ppermute | solution.py:32
  18.8 4.7 %collective-permute-start.4 = (bf16[96,576]{0,1:T(8,128)(2,1)S(1)}, bf16[96,576]{0,1:T(8,128)(2,1)S(1)}, u32[]{:S(2)}, u32[]{:S(2)}) collective-permute-start(bf16[96,576]{0,1:T(8,128)(2,1)S(1)} %pad_maximum_fusion.2), channel_id=1, source_target_pairs={{0,2},{1,3},{2,0},{3,1},{4,6},{5,7},{6,4},{7,5},{8,10},{9,11},{10,... | collective-permute-start | bytes 331784 | tf_op jit(solution)/shard_map/ppermute | solution.py:32
  23.5 0.8 constant_dynamic-update-slice_fusion
  25.0 0.8 slice_dynamic-update-slice_fusion.2
  25.8 1.5 collective-permute-done.5
  27.2 4.6 %collective-permute-done.4 = bf16[96,576]{0,1:T(8,128)(2,1)S(1)} collective-permute-done((bf16[96,576]{0,1:T(8,128)(2,1)S(1)}, bf16[96,576]{0,1:T(8,128)(2,1)S(1)}, u32[]{:S(2)}, u32[]{:S(2)}) %collective-permute-start.4) | collective-permute-done | bytes 110624 | tf_op jit(solution)/shard_map/ppermute | solution.py:32
  32.2 0.8 copy.52
  33.6 1.6 collective-permute-start.7
  35.1 1.5 collective-permute-start.6
  37.0 1.8 collective-permute-start
  38.7 7.7 %collective-permute-done.7.refs_2_ = bf16[96,2304]{1,0:T(8,128)(2,1)S(1)} collective-permute-done((bf16[96,2304]{1,0:T(8,128)(2,1)S(1)}, bf16[96,2304]{1,0:T(8,128)(2,1)S(1)}, u32[]{:S(2)}, u32[]{:S(2)}) %collective-permute-start.7) | collective-permute-done | bytes 442400 | tf_op jit(solution)/shard_map/ppermute | solution.py:28
  46.4 1.5 collective-permute-start.8
  47.9 6.3 %collective-permute-done.1 = bf16[120,768]{1,0:T(8,128)(2,1)S(1)} collective-permute-done((bf16[120,768]{1,0:T(8,128)(2,1)S(1)}, bf16[120,768]{1,0:T(8,128)(2,1)S(1)}, u32[]{:S(2)}, u32[]{:S(2)}) %collective-permute-start.1) | collective-permute-done | bytes 184352 | tf_op jit(solution)/shard_map/ppermute | solution.py:32
  56.7 1.7 collective-permute-done.11.refs_6_
  59.3 10.4 %project.1 = (bf16[1024,2304]{1,0:T(8,128)(2,1)}, bf16[8,96,2304]{2,1,0:T(8,128)(2,1)}) custom-call(s32[8]{0:T(128)S(1)} %concatenate.35.order.order_ref, bf16[1024,768]{1,0:T(8,128)(2,1)} %refs_0_.1, f32[1,2304]{1,0:T(1,128)S(1)} %fusion.7.bias, bf16[96,2304]{1,0:T(8,128)(2,1)S(1)} %reshape.158.refs_0_, bf16[96,2304]{1,0:T(8,128)(2,1)} %collective-permute-done.6.refs_1_, ...), custom_call_target="tpu_custom_call" | custom-call | flops 3623878656 | bytes 13369344 | tf_op jit(solution)/shard_map/project/pallas_call | solution.py:152
  69.8 4.0 %collective-permute-done.14.refs_2_ = bf16[480,768]{1,0:T(8,128)(2,1)S(1)} collective-permute-done((bf16[480,768]{1,0:T(8,128)(2,1)S(1)}, bf16[480,768]{1,0:T(8,128)(2,1)S(1)}, u32[]{:S(2)}, u32[]{:S(2)}) %collective-permute-start.14) | collective-permute-done | bytes 737312 | tf_op jit(solution)/shard_map/ppermute | solution.py:28
  73.8 2.1 collective-permute-done.13.refs_1_
  75.9 1.2 collective-permute-start.18
  78.2 10.8 %attend_forward.2 = (bf16[1024,768]{1,0:T(8,128)(2,1)}, f32[2,6,2,512]{3,2,1,0:T(2,128)}) custom-call(s32[2]{0:T(128)} %dynamic_slice.42.kinds, bf16[1024,2304]{1,0:T(8,128)(2,1)} %get-tuple-element.99.query_ref.key_ref.value_ref.refs_0_.refs_1_.refs_2_, bf16[1024,2304]{1,0:T(8,128)(2,1)} %get-tuple-element.99.query_ref.key_ref.value_ref.refs_0_.refs_1_.refs_2_, ...), custom_call_target="tpu_custom_call" | custom-call | flops 3221225472 | bytes 3145728 | tf_op jit(solution)/shard_map/attend_forward/pallas_call | solution.py:557
  89.0 4.7 %collective-permute-done.18.refs_3_ = bf16[480,768]{1,0:T(8,128)(2,1)} collective-permute-done((bf16[480,768]{1,0:T(8,128)(2,1)S(1)}, bf16[480,768]{1,0:T(8,128)(2,1)}, u32[]{:S(2)}, u32[]{:S(2)}) %collective-permute-start.18) | collective-permute-done | bytes 737312 | tf_op jit(solution)/shard_map/ppermute | solution.py:28
  93.7 2.3 collective-permute-start.19
  96.3 10.9 %attend_forward.3 = (bf16[1024,768]{1,0:T(8,128)(2,1)}, f32[2,6,2,512]{3,2,1,0:T(2,128)}) custom-call(s32[2]{0:T(128)} %dynamic_slice.42.kinds, bf16[1024,2304]{1,0:T(8,128)(2,1)} %get-tuple-element.99.query_ref.key_ref.value_ref.refs_0_.refs_1_.refs_2_, ...), custom_call_target="tpu_custom_call", output_to_operand_aliasing={{0}: (4, {}), {1}: (5, {})} | custom-call | flops 3221225472 | bytes 3145728 | tf_op jit(solution)/shard_map/attend_forward/pallas_call | solution.py:557
  107.3 41.6 %dense.1 = (bf16[1024,768]{1,0:T(8,128)(2,1)}, bf16[1024,3072]{1,0:T(8,128)(2,1)}, bf16[1024,768]{1,0:T(8,128)(2,1)}, bf16[1024,768]{1,0:T(8,128)(2,1)}, bf16[10...) custom-call(s32[2]{0:T(128)S(1)} %copy-done.2, ...), custom_call_target="tpu_custom_call" | custom-call | flops 21743271936 | bytes 28311552 | tf_op jit(solution)/shard_map/dense/pallas_call | solution.py:696
  148.9 1.4 copy-done
  150.3 5.4 %columns_term.2 = bf16[4,384,768]{2,1,0:T(8,128)(2,1)S(1)} custom-call(s32[4]{0:T(128)S(1)} %add_xor_fusion.order, bf16[1024,3072]{1,0:T(8,128)(2,1)} %get-tuple-element.112.left, bf16[1024,768]{1,0:T(8,128)(2,1)S(1)} %copy-done), custom_call_target="tpu_custom_call" | custom-call | flops 2415919104 | bytes 7077888 | tf_op jit(solution)/shard_map/columns_term/pallas_call | solution.py:252
  155.7 7.6 %collective-permute-start.20 = (bf16[4,384,768]{2,1,0:T(8,128)(2,1)S(1)}, bf16[4,384,768]{2,1,0:T(8,128)(2,1)S(1)}, u32[]{:S(2)}, u32[]{:S(2)}) collective-permute-start(bf16[4,384,768]{2,1,0:T(8,128)(2,1)S(1)} %columns_term.2), channel_id=1, source_target_pairs={{0,4},{4,0},{8,12},{12,8},{16,20},{20,16},{24,28},{28,24},{1,5},{5... | collective-permute-start | bytes 7077896 | tf_op jit(solution)/shard_map/ppermute | solution.py:28
  163.4 5.6 %columns_term.3 = bf16[4,384,768]{2,1,0:T(8,128)(2,1)S(1)} custom-call(s32[4]{0:T(128)S(1)} %add_add_fusion.1.order, bf16[1024,3072]{1,0:T(8,128)(2,1)} %get-tuple-element.112.left, bf16[1024,768]{1,0:T(8,128)(2,1)S(1)} %copy-done), custom_call_target="tpu_custom_call" | custom-call | flops 2415919104 | bytes 7077888 | tf_op jit(solution)/shard_map/columns_term/pallas_call | solution.py:252
  169.3 1.0 collective-permute-start.21
  170.3 0.9 copy-done.1
  171.7 12.1 %rows_terms.2 = (bf16[4,96,3840]{2,1,0:T(8,128)(2,1)}, bf16[4,96,3840]{2,1,0:T(8,128)(2,1)}) custom-call(s32[8]{0:T(128)S(1)} %concatenate.35.order.order_ref, bf16[1024,768]{1,0:T(8,128)(2,1)S(1)} %copy-done.4, bf16[1024,768]{1,0:T(8,128)(2,1)S(1)} %copy-done.1, bf16[1024,3072]{1,0:T(8,128)(2,1)} %get-tuple-element.116.refs_2_, bf16[1024,768]{1,0:T(8,128)(2,1)S(1)} %copy-done.5), custom_call_target="tpu_custom_call" | custom-call | flops 6039797760 | bytes 13762560 | tf_op jit(solution)/shard_map/rows_terms/pallas_call | solution.py:225
  183.8 1.8 collective-permute-done.21
  185.8 0.8 copy-done.14
  186.6 14.0 %attend_backward.2 = (bf16[1024,768]{1,0:T(8,128)(2,1)}, bf16[1024,768]{1,0:T(8,128)(2,1)}, bf16[1024,768]{1,0:T(8,128)(2,1)}) custom-call(s32[2]{0:T(128)} %dynamic_slice.42.kinds, bf16[1024,2304]{1,0:T(8,128)(2,1)} %get-tuple-element.99.query_ref.key_ref.value_ref.refs_0_.refs_1_.refs_2_, ...), custom_call_target="tpu_custom_call" | custom-call | flops 8053063680 | bytes 6291456 | tf_op jit(solution)/shard_map/attend_backward/pallas_call | solution.py:557
  200.7 1.9 fusion.1
  203.1 7.5 %collective-permute-start.26 = (bf16[96,768]{1,0:T(8,128)(2,1)S(1)}, bf16[96,768]{1,0:T(8,128)(2,1)S(1)}, u32[]{:S(2)}, u32[]{:S(2)}) collective-permute-start(bf16[96,768]{1,0:T(8,128)(2,1)S(1)} %get-tuple-element.190), channel_id=1, source_target_pairs={{0,2},{1,3},{2,0},{3,1},{4,6},{5,7},{6,4},{7,5},{8,10},{9,11},{10,... | collective-permute-start | bytes 442376 | tf_op jit(solution)/shard_map/ppermute | solution.py:32
  210.6 2.9 add_convert_fusion
  213.4 2.3 collective-permute-start.24
  215.7 14.3 %attend_backward.3 = (bf16[1024,768]{1,0:T(8,128)(2,1)}, bf16[1024,768]{1,0:T(8,128)(2,1)}, bf16[1024,768]{1,0:T(8,128)(2,1)}) custom-call(s32[2]{0:T(128)} %dynamic_slice.42.kinds, bf16[1024,2304]{1,0:T(8,128)(2,1)} %get-tuple-element.99.query_ref.key_ref.value_ref.refs_0_.refs_1_.refs_2_, ...), custom_call_target="tpu_custom_call", output_to_operand_aliasing={{0}: (7, {}), {1}: (8, {}), {2}: (9, {})} | custom-call | flops 8053063680 | bytes 6291456 | tf_op jit(solution)/shard_map/attend_backward/pallas_call | solution.py:557
  230.0 0.8 convert_add_fusion.2
  230.8 4.1 %pad_maximum_fusion.refs_1_ = bf16[1024,2304]{1,0:T(8,128)(2,1)} fusion(bf16[1024,768]{1,0:T(8,128)(2,1)} %get-tuple-element.133, bf16[1024,768]{1,0:T(8,128)(2,1)} %get-tuple-element.132, bf16[1024,768]{1,0:T(8,128)(2,1)} %get-tuple-element.131), kind=kLoop, calls=%fused_computation | loop fusion | flops 14155776 | bytes 9437184 | tf_op jit(solution)/shard_map/concatenate | solution.py:819
  234.9 1.1 copy-done.12
  236.0 1.4 fusion.3
  237.4 7.5 %rows_terms.3 = (bf16[4,96,2304]{2,1,0:T(8,128)(2,1)S(1)}, bf16[4,96,2304]{2,1,0:T(8,128)(2,1)S(1)}) custom-call(s32[8]{0:T(128)S(1)} %concatenate.35.order.order_ref, bf16[1024,768]{1,0:T(8,128)(2,1)S(1)} %copy-done.3, bf16[1024,2304]{1,0:T(8,128)(2,1)} %pad_maximum_fusion.refs_1_), custom_call_target="tpu_custom_call" | custom-call | flops 3623878656 | bytes 8257536 | tf_op jit(solution)/shard_map/rows_terms/pallas_call | solution.py:225
  245.0 4.3 %collective-permute-start.28 = (bf16[4,96,2304]{2,1,0:T(8,128)(2,1)S(1)}, bf16[4,96,2304]{2,1,0:T(8,128)(2,1)S(1)}, u32[]{:S(2)}, u32[]{:S(2)}) collective-permute-start(bf16[4,96,2304]{2,1,0:T(8,128)(2,1)S(1)} %get-tuple-element.141), channel_id=1, source_target_pairs={{0,4},{4,0},{8,12},{12,8},{16,20},{20,16},{24,28},{28,24},{1,5},{5... | collective-permute-start | bytes 5308424 | tf_op jit(solution)/shard_map/ppermute | solution.py:28
  249.2 2.7 collective-permute-start.40
  252.5 8.9 %collective-permute-done.40 = bf16[96,3840]{1,0:T(8,128)(2,1)S(1)} collective-permute-done((bf16[96,3840]{1,0:T(8,128)(2,1)S(1)}, bf16[96,3840]{1,0:T(8,128)(2,1)S(1)}, u32[]{:S(2)}, u32[]{:S(2)}) %collective-permute-start.40) | collective-permute-done | bytes 737312 | tf_op jit(solution)/shard_map/ppermute | solution.py:28
  261.7 2.3 fusion
  264.2 3.4 %collective-permute-start.43 = (bf16[24,3840]{1,0:T(8,128)(2,1)S(1)}, bf16[24,3840]{1,0:T(8,128)(2,1)S(1)}, u32[]{:S(2)}, u32[]{:S(2)}) collective-permute-start(bf16[24,3840]{1,0:T(8,128)(2,1)S(1)} %get-tuple-element.180), channel_id=1, source_target_pairs={{0,3},{1,0},{2,1},{3,2},{4,7},{5,4},{6,5},{7,6},{8,11},{9,8},{10,9... | collective-permute-start | bytes 552968 | tf_op jit(solution)/shard_map/ppermute | solution.py:32
  268.3 2.1 collective-permute-start.36
  270.4 6.7 %convolution_add_fusion = f32[1024,768]{1,0:T(8,128)} fusion(f32[1024,768]{1,0:T(8,128)} %get-tuple-element.108, bf16[1024,2304]{1,0:T(8,128)(2,1)S(1)} %bitcast.84, bf16[768,2304]{1,0:T(8,128)(2,1)S(1)} %bitcast.100), kind=kOutput, calls=%fused_computation.6 | convolution fusion | flops 3624665088 | bytes 14548992 | tf_op jit(solution)/shard_map/dot_general | solution.py:457
  277.1 6.3 %collective-permute-done.42 = bf16[24,3840]{1,0:T(8,128)(2,1)S(1)} collective-permute-done((bf16[24,3840]{1,0:T(8,128)(2,1)S(1)}, bf16[24,3840]{1,0:T(8,128)(2,1)S(1)}, u32[]{:S(2)}, u32[]{:S(2)}) %collective-permute-start.42) | collective-permute-done | bytes 184352 | tf_op jit(solution)/shard_map/ppermute | solution.py:32
  283.5 2.8 collective-permute-start.38
  286.3 1.9 collective-permute-start.37
  290.3 1.9 collective-permute-done.37
  292.8 4.1 %collective-permute-done.31 = bf16[96,2304]{1,0:T(8,128)(2,1)} collective-permute-done((bf16[96,2304]{1,0:T(8,128)(2,1)S(1)}, bf16[96,2304]{1,0:T(8,128)(2,1)}, u32[]{:S(2)}, u32[]{:S(2)}) %collective-permute-start.31) | collective-permute-done | bytes 442400 | tf_op jit(solution)/shard_map/ppermute | solution.py:28
  296.9 1.4 fusion.2
  298.9 0.8 copy.57
  299.7 1.9 collective-permute-start.35
  303.0 3.0 collective-permute-done.35
  306.0 7.9 %collective-permute-done.34 = bf16[96,576]{0,1:T(8,128)(2,1)S(1)} collective-permute-done((bf16[96,576]{0,1:T(8,128)(2,1)S(1)}, bf16[96,576]{0,1:T(8,128)(2,1)S(1)}, u32[]{:S(2)}, u32[]{:S(2)}) %collective-permute-start.34) | collective-permute-done | bytes 110624 | tf_op jit(solution)/shard_map/ppermute | solution.py:32
  (167 shorter events, 17.3 us)
Async XLA Ops:
  7.2 100.1 %all-gather.2.cloned.1.call-start = ((), (), s32[]{:S(2)}) async-start(), calls=%async_computation | async-start | bytes 4866048 | tf_op jit(solution)/shard_map/all_gather | solution.py:296
  10.0 8.5 %collective-permute-start.3 = (bf16[96,576]{0,1:T(8,128)(2,1)S(1)}, bf16[96,576]{0,1:T(8,128)(2,1)S(1)}, u32[]{:S(2)}, u32[]{:S(2)}) collective-permute-start(bf16[96,576]{0,1:T(8,128)(2,1)S(1)} %pad_maximum_fusion.2), channel_id=1, source_target_pairs={{0,3},{1,0},{2,1},{3,2},{4,7},{5,4},{6,5},{7,6},{8,11},{9,8},{10,9... | collective-permute-start | bytes 331784 | tf_op jit(solution)/shard_map/ppermute | solution.py:32
  18.6 8.7 %collective-permute-start.5 = (bf16[96,576]{0,1:T(8,128)(2,1)S(1)}, bf16[96,576]{0,1:T(8,128)(2,1)S(1)}, u32[]{:S(2)}, u32[]{:S(2)}) collective-permute-start(bf16[96,576]{0,1:T(8,128)(2,1)S(1)} %pad_maximum_fusion.2), channel_id=1, source_target_pairs={{0,1},{1,2},{2,3},{3,0},{4,5},{5,6},{6,7},{7,4},{8,9},{9,10},{10,1... | collective-permute-start | bytes 331784 | tf_op jit(solution)/shard_map/ppermute | solution.py:32
  18.8 13.1 %collective-permute-start.4 = (bf16[96,576]{0,1:T(8,128)(2,1)S(1)}, bf16[96,576]{0,1:T(8,128)(2,1)S(1)}, u32[]{:S(2)}, u32[]{:S(2)}) collective-permute-start(bf16[96,576]{0,1:T(8,128)(2,1)S(1)} %pad_maximum_fusion.2), channel_id=1, source_target_pairs={{0,2},{1,3},{2,0},{3,1},{4,6},{5,7},{6,4},{7,5},{8,10},{9,11},{10,... | collective-permute-start | bytes 331784 | tf_op jit(solution)/shard_map/ppermute | solution.py:32
  33.5 23.1 %copy-start.17 = (bf16[768]{0:T(1024)(128)(2,1)S(1)}, bf16[768]{0:T(1024)(128)(2,1)}, u32[]{:S(2)}) copy-start(bf16[768]{0:T(1024)(128)(2,1)} %param.23) | copy-start | bytes 4612
  33.5 23.1 %copy-start.18 = (bf16[768]{0:T(1024)(128)(2,1)S(1)}, bf16[768]{0:T(1024)(128)(2,1)}, u32[]{:S(2)}) copy-start(bf16[768]{0:T(1024)(128)(2,1)} %param.24) | copy-start | bytes 4612
  33.6 12.8 %collective-permute-start.7 = (bf16[96,2304]{1,0:T(8,128)(2,1)S(1)}, bf16[96,2304]{1,0:T(8,128)(2,1)S(1)}, u32[]{:S(2)}, u32[]{:S(2)}) collective-permute-start(bf16[96,2304]{1,0:T(8,128)(2,1)S(1)} %reshape.158.refs_0_), channel_id=1, source_target_pairs={{0,16},{4,12},{8,24},{12,4},{16,0},{20,28},{24,8},{28,20},{1,17},{... | collective-permute-start | bytes 1327112 | tf_op jit(solution)/shard_map/ppermute | solution.py:28
  35.1 11.3 %collective-permute-start.6 = (bf16[96,2304]{1,0:T(8,128)(2,1)S(1)}, bf16[96,2304]{1,0:T(8,128)(2,1)}, u32[]{:S(2)}, u32[]{:S(2)}) collective-permute-start(bf16[96,2304]{1,0:T(8,128)(2,1)S(1)} %reshape.158.refs_0_), channel_id=1, source_target_pairs={{0,8},{4,20},{8,0},{12,28},{16,24},{20,4},{24,16},{28,12},{1,9},{5... | collective-permute-start | bytes 1327112 | tf_op jit(solution)/shard_map/ppermute | solution.py:28
  36.7 11.3 %collective-permute-start.2 = (bf16[120,768]{1,0:T(8,128)(2,1)S(1)}, bf16[120,768]{1,0:T(8,128)(2,1)S(1)}, u32[]{:S(2)}, u32[]{:S(2)}) collective-permute-start(bf16[120,768]{1,0:T(8,128)(2,1)S(1)} %slice_dynamic-update-slice_fusion), channel_id=1, source_target_pairs={{0,3},{1,0},{2,1},{3,2},{4,7},{5,4},{6,5},{7,6},{8,11},{9,8},{10,9... | collective-permute-start | bytes 552968 | tf_op jit(solution)/shard_map/ppermute | solution.py:32
  37.0 17.3 %collective-permute-start.1 = (bf16[120,768]{1,0:T(8,128)(2,1)S(1)}, bf16[120,768]{1,0:T(8,128)(2,1)S(1)}, u32[]{:S(2)}, u32[]{:S(2)}) collective-permute-start(bf16[120,768]{1,0:T(8,128)(2,1)S(1)} %slice_dynamic-update-slice_fusion), channel_id=1, source_target_pairs={{0,2},{1,3},{2,0},{3,1},{4,6},{5,7},{6,4},{7,5},{8,10},{9,11},{10,... | collective-permute-start | bytes 552968 | tf_op jit(solution)/shard_map/ppermute | solution.py:32
  37.0 17.3 %collective-permute-start = (bf16[120,768]{1,0:T(8,128)(2,1)S(1)}, bf16[120,768]{1,0:T(8,128)(2,1)S(1)}, u32[]{:S(2)}, u32[]{:S(2)}) collective-permute-start(bf16[120,768]{1,0:T(8,128)(2,1)S(1)} %slice_dynamic-update-slice_fusion), channel_id=1, source_target_pairs={{0,1},{1,2},{2,3},{3,0},{4,5},{5,6},{6,7},{7,4},{8,9},{9,10},{10,1... | collective-permute-start | bytes 552968 | tf_op jit(solution)/shard_map/ppermute | solution.py:32
  46.4 9.5 %collective-permute-start.9 = (bf16[96,2304]{1,0:T(8,128)(2,1)S(1)}, bf16[96,2304]{1,0:T(8,128)(2,1)}, u32[]{:S(2)}, u32[]{:S(2)}) collective-permute-start(bf16[96,2304]{1,0:T(8,128)(2,1)S(1)} %reshape.158.refs_0_), channel_id=1, source_target_pairs={{0,4},{4,0},{8,12},{12,8},{16,20},{20,16},{24,28},{28,24},{1,5},{5... | collective-permute-start | bytes 1327112 | tf_op jit(solution)/shard_map/ppermute | solution.py:28
  46.4 10.0 %collective-permute-start.8 = (bf16[96,2304]{1,0:T(8,128)(2,1)}, bf16[96,2304]{1,0:T(8,128)(2,1)}, u32[]{:S(2)}, u32[]{:S(2)}) collective-permute-start(bf16[96,2304]{1,0:T(8,128)(2,1)} %collective-permute-done.6.refs_1_), channel_id=1, source_target_pairs={{0,16},{4,12},{8,24},{12,4},{16,0},{20,28},{24,8},{28,20},{1,17},{... | collective-permute-start | bytes 1327112 | tf_op jit(solution)/shard_map/ppermute | solution.py:28
  54.5 19.3 %collective-permute-start.14 = (bf16[480,768]{1,0:T(8,128)(2,1)S(1)}, bf16[480,768]{1,0:T(8,128)(2,1)S(1)}, u32[]{:S(2)}, u32[]{:S(2)}) collective-permute-start(bf16[480,768]{1,0:T(8,128)(2,1)S(1)} %bitcast.79), channel_id=1, source_target_pairs={{0,16},{4,12},{8,24},{12,4},{16,0},{20,28},{24,8},{28,20},{1,17},{... | collective-permute-start | bytes 2211848 | tf_op jit(solution)/shard_map/ppermute | solution.py:28
  55.2 20.7 %collective-permute-start.13 = (bf16[480,768]{1,0:T(8,128)(2,1)S(1)}, bf16[480,768]{1,0:T(8,128)(2,1)S(1)}, u32[]{:S(2)}, u32[]{:S(2)}) collective-permute-start(bf16[480,768]{1,0:T(8,128)(2,1)S(1)} %bitcast.80), channel_id=1, source_target_pairs={{0,8},{4,20},{8,0},{12,28},{16,24},{20,4},{24,16},{28,12},{1,9},{5... | collective-permute-start | bytes 2211848 | tf_op jit(solution)/shard_map/ppermute | solution.py:28
  55.9 2.5 collective-permute-start.11
  55.9 2.8 collective-permute-start.10
  56.4 2.9 collective-permute-start.12
  56.7 20.8 %copy-start.26 = (s32[8]{0:T(128)S(1)}, s32[8]{0:T(128)}, u32[]{:S(2)}) copy-start(s32[8]{0:T(128)} %param.19) | copy-start | bytes 100
  58.4 30.6 %collective-permute-start.15 = (bf16[480,768]{1,0:T(8,128)(2,1)S(1)}, bf16[480,768]{1,0:T(8,128)(2,1)}, u32[]{:S(2)}, u32[]{:S(2)}) collective-permute-start(bf16[480,768]{1,0:T(8,128)(2,1)S(1)} %bitcast.81), channel_id=1, source_target_pairs={{0,4},{4,0},{8,12},{12,8},{16,20},{20,16},{24,28},{28,24},{1,5},{5... | collective-permute-start | bytes 2211848 | tf_op jit(solution)/shard_map/ppermute | solution.py:28
  75.9 17.8 %collective-permute-start.18 = (bf16[480,768]{1,0:T(8,128)(2,1)S(1)}, bf16[480,768]{1,0:T(8,128)(2,1)}, u32[]{:S(2)}, u32[]{:S(2)}) collective-permute-start(bf16[480,768]{1,0:T(8,128)(2,1)S(1)} %collective-permute-done.13.refs_1_), channel_id=1, source_target_pairs={{0,16},{4,12},{8,24},{12,4},{16,0},{20,28},{24,8},{28,20},{1,17},{... | collective-permute-start | bytes 2211848 | tf_op jit(solution)/shard_map/ppermute | solution.py:28
  77.1 16.6 %collective-permute-start.16 = (bf16[480,768]{1,0:T(8,128)(2,1)S(1)}, bf16[480,768]{1,0:T(8,128)(2,1)S(1)}, u32[]{:S(2)}, u32[]{:S(2)}) collective-permute-start(bf16[480,768]{1,0:T(8,128)(2,1)S(1)} %collective-permute-done.13.refs_1_), channel_id=1, source_target_pairs={{0,4},{4,0},{8,12},{12,8},{16,20},{20,16},{24,28},{28,24},{1,5},{5... | collective-permute-start | bytes 2211848 | tf_op jit(solution)/shard_map/ppermute | solution.py:28
  77.1 16.6 %collective-permute-start.17 = (bf16[480,768]{1,0:T(8,128)(2,1)S(1)}, bf16[480,768]{1,0:T(8,128)(2,1)}, u32[]{:S(2)}, u32[]{:S(2)}) collective-permute-start(bf16[480,768]{1,0:T(8,128)(2,1)S(1)} %collective-permute-done.14.refs_2_), channel_id=1, source_target_pairs={{0,4},{4,0},{8,12},{12,8},{16,20},{20,16},{24,28},{28,24},{1,5},{5... | collective-permute-start | bytes 2211848 | tf_op jit(solution)/shard_map/ppermute | solution.py:28
  78.2 17.8 %copy-start.19 = (bf16[768]{0:T(1024)(128)(2,1)S(1)}, bf16[768]{0:T(1024)(128)(2,1)}, u32[]{:S(2)}) copy-start(bf16[768]{0:T(1024)(128)(2,1)} %param.26) | copy-start | bytes 4612
  78.2 17.8 %copy-start.20 = (bf16[768]{0:T(1024)(128)(2,1)S(1)}, bf16[768]{0:T(1024)(128)(2,1)}, u32[]{:S(2)}) copy-start(bf16[768]{0:T(1024)(128)(2,1)} %param.27) | copy-start | bytes 4612
  78.2 17.8 %copy-start.21 = (bf16[768]{0:T(1024)(128)(2,1)S(1)}, bf16[768]{0:T(1024)(128)(2,1)}, u32[]{:S(2)}) copy-start(bf16[768]{0:T(1024)(128)(2,1)} %param.28) | copy-start | bytes 4612
  78.2 17.9 %copy-start.22 = (bf16[768]{0:T(1024)(128)(2,1)S(1)}, bf16[768]{0:T(1024)(128)(2,1)}, u32[]{:S(2)}) copy-start(bf16[768]{0:T(1024)(128)(2,1)} %param.32) | copy-start | bytes 4612
  78.2 17.9 %copy-start.23 = (bf16[768]{0:T(1024)(128)(2,1)S(1)}, bf16[768]{0:T(1024)(128)(2,1)}, u32[]{:S(2)}) copy-start(bf16[768]{0:T(1024)(128)(2,1)} %param.33) | copy-start | bytes 4612
  78.2 17.9 %copy-start.24 = (bf16[768]{0:T(1024)(128)(2,1)S(1)}, bf16[768]{0:T(1024)(128)(2,1)}, u32[]{:S(2)}) copy-start(bf16[768]{0:T(1024)(128)(2,1)} %param.34) | copy-start | bytes 4612
  78.2 17.9 %copy-start.16 = (bf16[3072]{0:T(1024)(128)(2,1)S(1)}, bf16[3072]{0:T(1024)(128)(2,1)}, u32[]{:S(2)}) copy-start(bf16[3072]{0:T(1024)(128)(2,1)} %param.30) | copy-start | bytes 18436
  93.7 13.5 %collective-permute-start.19 = (bf16[480,768]{1,0:T(8,128)(2,1)}, bf16[480,768]{1,0:T(8,128)(2,1)}, u32[]{:S(2)}, u32[]{:S(2)}) collective-permute-start(bf16[480,768]{1,0:T(8,128)(2,1)} %collective-permute-done.18.refs_3_), channel_id=1, source_target_pairs={{0,4},{4,0},{8,12},{12,8},{16,20},{20,16},{24,28},{28,24},{1,5},{5... | collective-permute-start | bytes 2211848 | tf_op jit(solution)/shard_map/ppermute | solution.py:28
  96.3 10.9 %copy-start.2 = (s32[2]{0:T(128)S(1)}, s32[2]{0:T(128)}, u32[]{:S(2)}) copy-start(s32[2]{0:T(128)} %dynamic_slice.42.kinds) | copy-start | bytes 28
  155.7 13.3 %collective-permute-start.20 = (bf16[4,384,768]{2,1,0:T(8,128)(2,1)S(1)}, bf16[4,384,768]{2,1,0:T(8,128)(2,1)S(1)}, u32[]{:S(2)}, u32[]{:S(2)}) collective-permute-start(bf16[4,384,768]{2,1,0:T(8,128)(2,1)S(1)} %columns_term.2), channel_id=1, source_target_pairs={{0,4},{4,0},{8,12},{12,8},{16,20},{20,16},{24,28},{28,24},{1,5},{5... | collective-permute-start | bytes 7077896 | tf_op jit(solution)/shard_map/ppermute | solution.py:28
  169.0 16.6 %copy-start.10 = (bf16[4,384,768]{2,1,0:T(8,128)(2,1)}, bf16[4,384,768]{2,1,0:T(8,128)(2,1)S(1)}, u32[]{:S(2)}) copy-start(bf16[4,384,768]{2,1,0:T(8,128)(2,1)S(1)} %collective-permute-done.20) | copy-start | bytes 7077892
  169.3 16.3 %collective-permute-start.21 = (bf16[2,384,768]{2,1,0:T(8,128)(2,1)S(1)}, bf16[2,384,768]{2,1,0:T(8,128)(2,1)S(1)}, u32[]{:S(2)}, u32[]{:S(2)}) collective-permute-start(bf16[2,384,768]{2,1,0:T(8,128)(2,1)S(1)} %add_convert_fusion.1), channel_id=1, source_target_pairs={{0,16},{4,12},{8,24},{12,4},{16,0},{20,28},{24,8},{28,20},{1,17},{... | collective-permute-start | bytes 3538952 | tf_op jit(solution)/shard_map/ppermute | solution.py:28
  186.6 23.9 %collective-permute-start.23 = (bf16[4,96,3840]{2,1,0:T(8,128)(2,1)}, bf16[4,96,3840]{2,1,0:T(8,128)(2,1)}, u32[]{:S(2)}, u32[]{:S(2)}) collective-permute-start(bf16[4,96,3840]{2,1,0:T(8,128)(2,1)} %get-tuple-element.126), channel_id=1, source_target_pairs={{0,4},{4,0},{8,12},{12,8},{16,20},{20,16},{24,28},{28,24},{1,5},{5... | collective-permute-start | bytes 8847368 | tf_op jit(solution)/shard_map/ppermute | solution.py:28
  186.6 14.1 %collective-permute-start.22 = (bf16[384,768]{1,0:T(8,128)(2,1)S(1)}, bf16[384,768]{1,0:T(8,128)(2,1)}, u32[]{:S(2)}, u32[]{:S(2)}) collective-permute-start(bf16[384,768]{1,0:T(8,128)(2,1)S(1)} %fusion.4), channel_id=1, source_target_pairs={{0,8},{4,20},{8,0},{12,28},{16,24},{20,4},{24,16},{28,12},{1,9},{5... | collective-permute-start | bytes 1769480 | tf_op jit(solution)/shard_map/ppermute | solution.py:28
  200.7 9.9 %copy-start.8 = (bf16[4,96,3840]{2,1,0:T(8,128)(2,1)S(1)}, bf16[4,96,3840]{2,1,0:T(8,128)(2,1)}, u32[]{:S(2)}) copy-start(bf16[4,96,3840]{2,1,0:T(8,128)(2,1)} %get-tuple-element.118) | copy-start | bytes 8847364
  202.6 27.4 %collective-permute-start.27 = (bf16[96,768]{1,0:T(8,128)(2,1)S(1)}, bf16[96,768]{1,0:T(8,128)(2,1)S(1)}, u32[]{:S(2)}, u32[]{:S(2)}) collective-permute-start(bf16[96,768]{1,0:T(8,128)(2,1)S(1)} %get-tuple-element.192), channel_id=1, source_target_pairs={{0,3},{1,0},{2,1},{3,2},{4,7},{5,4},{6,5},{7,6},{8,11},{9,8},{10,9... | collective-permute-start | bytes 442376 | tf_op jit(solution)/shard_map/ppermute | solution.py:32
  203.1 26.9 %collective-permute-start.26 = (bf16[96,768]{1,0:T(8,128)(2,1)S(1)}, bf16[96,768]{1,0:T(8,128)(2,1)S(1)}, u32[]{:S(2)}, u32[]{:S(2)}) collective-permute-start(bf16[96,768]{1,0:T(8,128)(2,1)S(1)} %get-tuple-element.190), channel_id=1, source_target_pairs={{0,2},{1,3},{2,0},{3,1},{4,6},{5,7},{6,4},{7,5},{8,10},{9,11},{10,... | collective-permute-start | bytes 442376 | tf_op jit(solution)/shard_map/ppermute | solution.py:32
  210.6 19.4 %collective-permute-start.25 = (bf16[96,768]{1,0:T(8,128)(2,1)S(1)}, bf16[96,768]{1,0:T(8,128)(2,1)S(1)}, u32[]{:S(2)}, u32[]{:S(2)}) collective-permute-start(bf16[96,768]{1,0:T(8,128)(2,1)S(1)} %get-tuple-element.191), channel_id=1, source_target_pairs={{0,1},{1,2},{2,3},{3,0},{4,5},{5,6},{6,7},{7,4},{8,9},{9,10},{10,1... | collective-permute-start | bytes 442376 | tf_op jit(solution)/shard_map/ppermute | solution.py:32
  213.4 21.5 %collective-permute-start.24 = (bf16[2,96,3840]{2,1,0:T(8,128)(2,1)}, bf16[2,96,3840]{2,1,0:T(8,128)(2,1)S(1)}, u32[]{:S(2)}, u32[]{:S(2)}) collective-permute-start(bf16[2,96,3840]{2,1,0:T(8,128)(2,1)} %add_convert_fusion), channel_id=1, source_target_pairs={{0,16},{4,12},{8,24},{12,4},{16,0},{20,28},{24,8},{28,20},{1,17},{... | collective-permute-start | bytes 4423688 | tf_op jit(solution)/shard_map/ppermute | solution.py:28
  237.4 14.5 %copy-start.6 = (bf16[1024,768]{1,0:T(8,128)(2,1)S(1)}, bf16[1024,768]{1,0:T(8,128)(2,1)}, u32[]{:S(2)}) copy-start(bf16[1024,768]{1,0:T(8,128)(2,1)} %get-tuple-element.131) | copy-start | bytes 4718596
  237.4 14.5 %copy-start.7 = (bf16[1024,768]{1,0:T(8,128)(2,1)S(1)}, bf16[1024,768]{1,0:T(8,128)(2,1)}, u32[]{:S(2)}) copy-start(bf16[1024,768]{1,0:T(8,128)(2,1)} %get-tuple-element.133) | copy-start | bytes 4718596
  245.0 16.4 %collective-permute-start.28 = (bf16[4,96,2304]{2,1,0:T(8,128)(2,1)S(1)}, bf16[4,96,2304]{2,1,0:T(8,128)(2,1)S(1)}, u32[]{:S(2)}, u32[]{:S(2)}) collective-permute-start(bf16[4,96,2304]{2,1,0:T(8,128)(2,1)S(1)} %get-tuple-element.141), channel_id=1, source_target_pairs={{0,4},{4,0},{8,12},{12,8},{16,20},{20,16},{24,28},{28,24},{1,5},{5... | collective-permute-start | bytes 5308424 | tf_op jit(solution)/shard_map/ppermute | solution.py:28
  249.2 12.2 %collective-permute-start.40 = (bf16[96,3840]{1,0:T(8,128)(2,1)S(1)}, bf16[96,3840]{1,0:T(8,128)(2,1)S(1)}, u32[]{:S(2)}, u32[]{:S(2)}) collective-permute-start(bf16[96,3840]{1,0:T(8,128)(2,1)S(1)} %fusion.3), channel_id=1, source_target_pairs={{0,8},{4,20},{8,0},{12,28},{16,24},{20,4},{24,16},{28,12},{1,9},{5... | collective-permute-start | bytes 2211848 | tf_op jit(solution)/shard_map/ppermute | solution.py:28
  252.0 18.5 %slice-start = ((s8[4718592]{0:T(1024)(128)(4,1)}), s8[524288]{0:T(1024)(128)(4,1)S(1)}, s32[]{:S(2)}) async-start(s8[4718592]{0:T(1024)(128)(4,1)} %bitcast.83), calls=%async_computation.1 | async-start | bytes 1048576
  252.0 18.5 %copy-start.27 = (bf16[8,96,2304]{2,1,0:T(8,128)(2,1)S(1)}, bf16[8,96,2304]{2,1,0:T(8,128)(2,1)}, u32[]{:S(2)}) copy-start(bf16[8,96,2304]{2,1,0:T(8,128)(2,1)} %get-tuple-element.143) | copy-start | bytes 10616836
  252.4 9.3 %copy-start.13 = (bf16[2,96,3840]{2,1,0:T(8,128)(2,1)S(1)}, bf16[2,96,3840]{2,1,0:T(8,128)(2,1)}, u32[]{:S(2)}) copy-start(bf16[2,96,3840]{2,1,0:T(8,128)(2,1)} %copy-done.12) | copy-start | bytes 4423684
  261.4 26.9 %copy-start.11 = (bf16[4,96,2304]{2,1,0:T(8,128)(2,1)}, bf16[4,96,2304]{2,1,0:T(8,128)(2,1)S(1)}, u32[]{:S(2)}) copy-start(bf16[4,96,2304]{2,1,0:T(8,128)(2,1)S(1)} %collective-permute-done.28) | copy-start | bytes 5308420
  261.6 2.4 collective-permute-start.30
  264.1 4.2 %collective-permute-start.32 = (f32[12,768]{1,0:T(8,128)S(1)}, f32[12,768]{1,0:T(8,128)S(1)}, u32[]{:S(2)}, u32[]{:S(2)}) collective-permute-start(f32[12,768]{1,0:T(8,128)S(1)} %add.210), channel_id=1, source_target_pairs={{0,16},{4,12},{8,24},{12,4},{16,0},{20,28},{24,8},{28,20},{1,17},{... | collective-permute-start | bytes 110600 | tf_op jit(solution)/shard_map/ppermute | solution.py:28
  264.2 12.9 %collective-permute-start.43 = (bf16[24,3840]{1,0:T(8,128)(2,1)S(1)}, bf16[24,3840]{1,0:T(8,128)(2,1)S(1)}, u32[]{:S(2)}, u32[]{:S(2)}) collective-permute-start(bf16[24,3840]{1,0:T(8,128)(2,1)S(1)} %get-tuple-element.180), channel_id=1, source_target_pairs={{0,3},{1,0},{2,1},{3,2},{4,7},{5,4},{6,5},{7,6},{8,11},{9,8},{10,9... | collective-permute-start | bytes 552968 | tf_op jit(solution)/shard_map/ppermute | solution.py:32
  267.6 15.8 %collective-permute-start.42 = (bf16[24,3840]{1,0:T(8,128)(2,1)S(1)}, bf16[24,3840]{1,0:T(8,128)(2,1)S(1)}, u32[]{:S(2)}, u32[]{:S(2)}) collective-permute-start(bf16[24,3840]{1,0:T(8,128)(2,1)S(1)} %get-tuple-element.181), channel_id=1, source_target_pairs={{0,2},{1,3},{2,0},{3,1},{4,6},{5,7},{6,4},{7,5},{8,10},{9,11},{10,... | collective-permute-start | bytes 552968 | tf_op jit(solution)/shard_map/ppermute | solution.py:32
  267.6 15.8 %collective-permute-start.41 = (bf16[24,3840]{1,0:T(8,128)(2,1)S(1)}, bf16[24,3840]{1,0:T(8,128)(2,1)S(1)}, u32[]{:S(2)}, u32[]{:S(2)}) collective-permute-start(bf16[24,3840]{1,0:T(8,128)(2,1)S(1)} %get-tuple-element.182), channel_id=1, source_target_pairs={{0,1},{1,2},{2,3},{3,0},{4,5},{5,6},{6,7},{7,4},{8,9},{9,10},{10,1... | collective-permute-start | bytes 552968 | tf_op jit(solution)/shard_map/ppermute | solution.py:32
  268.2 20.0 %collective-permute-start.29 = (bf16[2,96,2304]{2,1,0:T(8,128)(2,1)S(1)}, bf16[2,96,2304]{2,1,0:T(8,128)(2,1)S(1)}, u32[]{:S(2)}, u32[]{:S(2)}) collective-permute-start(bf16[2,96,2304]{2,1,0:T(8,128)(2,1)S(1)} %add_convert_fusion.2), channel_id=1, source_target_pairs={{0,16},{4,12},{8,24},{12,4},{16,0},{20,28},{24,8},{28,20},{1,17},{... | collective-permute-start | bytes 2654216 | tf_op jit(solution)/shard_map/ppermute | solution.py:28
  268.3 15.1 %collective-permute-start.36 = (f32[12,768]{1,0:T(8,128)S(1)}, f32[12,768]{1,0:T(8,128)S(1)}, u32[]{:S(2)}, u32[]{:S(2)}) collective-permute-start(f32[12,768]{1,0:T(8,128)S(1)} %add.215), channel_id=1, source_target_pairs={{0,8},{4,20},{8,0},{12,28},{16,24},{20,4},{24,16},{28,12},{1,9},{5... | collective-permute-start | bytes 110600 | tf_op jit(solution)/shard_map/ppermute | solution.py:28
  283.4 6.9 %collective-permute-start.39 = (f32[12,768]{1,0:T(8,128)S(1)}, f32[12,768]{1,0:T(8,128)S(1)}, u32[]{:S(2)}, u32[]{:S(2)}) collective-permute-start(f32[12,768]{1,0:T(8,128)S(1)} %add.217), channel_id=1, source_target_pairs={{0,3},{1,0},{2,1},{3,2},{4,7},{5,4},{6,5},{7,6},{8,11},{9,8},{10,9... | collective-permute-start | bytes 110600 | tf_op jit(solution)/shard_map/ppermute | solution.py:32
  283.5 6.9 %collective-permute-start.38 = (f32[12,768]{1,0:T(8,128)S(1)}, f32[12,768]{1,0:T(8,128)S(1)}, u32[]{:S(2)}, u32[]{:S(2)}) collective-permute-start(f32[12,768]{1,0:T(8,128)S(1)} %add.217), channel_id=1, source_target_pairs={{0,2},{1,3},{2,0},{3,1},{4,6},{5,7},{6,4},{7,5},{8,10},{9,11},{10,... | collective-permute-start | bytes 110600 | tf_op jit(solution)/shard_map/ppermute | solution.py:32
  286.3 5.9 %collective-permute-start.37 = (f32[12,768]{1,0:T(8,128)S(1)}, f32[12,768]{1,0:T(8,128)S(1)}, u32[]{:S(2)}, u32[]{:S(2)}) collective-permute-start(f32[12,768]{1,0:T(8,128)S(1)} %add.217), channel_id=1, source_target_pairs={{0,1},{1,2},{2,3},{3,0},{4,5},{5,6},{6,7},{7,4},{8,9},{9,10},{10,1... | collective-permute-start | bytes 110600 | tf_op jit(solution)/shard_map/ppermute | solution.py:32
  288.4 8.5 %collective-permute-start.31 = (bf16[96,2304]{1,0:T(8,128)(2,1)S(1)}, bf16[96,2304]{1,0:T(8,128)(2,1)}, u32[]{:S(2)}, u32[]{:S(2)}) collective-permute-start(bf16[96,2304]{1,0:T(8,128)(2,1)S(1)} %fusion.5), channel_id=1, source_target_pairs={{0,8},{4,20},{8,0},{12,28},{16,24},{20,4},{24,16},{28,12},{1,9},{5... | collective-permute-start | bytes 1327112 | tf_op jit(solution)/shard_map/ppermute | solution.py:28
  299.7 6.2 %collective-permute-start.35 = (bf16[96,576]{0,1:T(8,128)(2,1)S(1)}, bf16[96,576]{0,1:T(8,128)(2,1)S(1)}, u32[]{:S(2)}, u32[]{:S(2)}) collective-permute-start(bf16[96,576]{0,1:T(8,128)(2,1)S(1)} %get-tuple-element.187), channel_id=1, source_target_pairs={{0,3},{1,0},{2,1},{3,2},{4,7},{5,4},{6,5},{7,6},{8,11},{9,8},{10,9... | collective-permute-start | bytes 331784 | tf_op jit(solution)/shard_map/ppermute | solution.py:32
  301.7 12.2 %collective-permute-start.34 = (bf16[96,576]{0,1:T(8,128)(2,1)S(1)}, bf16[96,576]{0,1:T(8,128)(2,1)S(1)}, u32[]{:S(2)}, u32[]{:S(2)}) collective-permute-start(bf16[96,576]{0,1:T(8,128)(2,1)S(1)} %get-tuple-element.188), channel_id=1, source_target_pairs={{0,2},{1,3},{2,0},{3,1},{4,6},{5,7},{6,4},{7,5},{8,10},{9,11},{10,... | collective-permute-start | bytes 331784 | tf_op jit(solution)/shard_map/ppermute | solution.py:32
  301.7 12.2 %collective-permute-start.33 = (bf16[96,576]{0,1:T(8,128)(2,1)S(1)}, bf16[96,576]{0,1:T(8,128)(2,1)S(1)}, u32[]{:S(2)}, u32[]{:S(2)}) collective-permute-start(bf16[96,576]{0,1:T(8,128)(2,1)S(1)} %get-tuple-element.189), channel_id=1, source_target_pairs={{0,1},{1,2},{2,3},{3,0},{4,5},{5,6},{6,7},{7,4},{8,9},{9,10},{10,1... | collective-permute-start | bytes 331784 | tf_op jit(solution)/shard_map/ppermute | solution.py:32
  (11 other events, 39.2 us)
Sparse Core Ops, SparseCore 0:
  18.7 80.6 all-gather.1
